TPU v7x, 512 devices: a whole 4x4x16 slice. The times are simulated.
512 devices in a mesh: space: 64 (over x_hi, z, core), sub: 8 (over y, x_lo).
Axes of the slice: x: 4 (x_hi: 2, x_lo: 2; x = x_hi * 2 + x_lo), y: 4, z: 16, core: 2. Of those that a mesh axis runs over, the one named last changes fastest.
Arguments:
- positions: float32 [3, 128, 16, 3, 128], P(None, 'space', 'sub'), may hold values from 0 to 1
- charges: float32 [128, 16, 3, 128], P('space', 'sub'), may hold values from -0.6 to 0.6
- counts: int32 [128, 16, 3], P('space', 'sub'), may hold values from 64 to 128
Outputs:
- forces: float32 [3, 128, 16, 3, 128], P(None, 'space', 'sub')
Inputs may be any that keep to these rules, and one draw needn't show every extreme that they name: `counts`: slots 0 to count - 1 of a cell hold atoms; the others are padding.
All inputs are finite; a program needn't handle non-finite values.
Results may differ from a plain program's by a relative error of at most 0.0003.
Values sent between devices are 32-bit elements; how exact they have to be, the bound alone decides.
A program may use at most 64 MiB of HBM per device.

v0:
```python
import math

import jax
import jax.numpy as jnp
from jax import lax
from jax.sharding import PartitionSpec as P

POINTS = 4
REACH = 4


SOFT_SQUARE = 0.0625
SPLIT_RATE = 0.8
FINE_WIDTHS = (1.0, 2.0)
FINE_WEIGHTS = (2.0, 0.5)
COARSE_FRACTIONS = (8.0, 4.0)
COARSE_WEIGHTS = (4.0, 2.0)
HIGHEST = lax.Precision.HIGHEST


def extended_2(value, sides, width):
    for axis, dim in sides:
        size, length = (lax.axis_size(axis), value.shape[dim])
        up = [(i, (i + 1) % size) for i in range(size)]
        down = [(j, i) for i, j in up]
        last = lax.slice_in_dim(value, length - width, length, axis=dim)
        first = lax.slice_in_dim(value, 0, width, axis=dim)
        before = lax.ppermute(last, axis, up)
        after = lax.ppermute(first, axis, down)
        value = jnp.concatenate([before, value, after], axis=dim)
    return value


def pair_force(own_pos, own_charge, other_pos, other_charge, offset_vec):
    shifted = own_pos - offset_vec.reshape((3,) + (1,) * (own_pos.ndim - 1))
    spread = shifted[..., :, None] - other_pos[..., None, :]
    square = jnp.sum(spread * spread, axis=0) + SOFT_SQUARE
    length = jnp.sqrt(square)
    factor = jax.scipy.special.erfc(SPLIT_RATE * length) / (square * length)
    factor = (
        factor
        + 2.0
        * SPLIT_RATE
        / math.sqrt(math.pi)
        * jnp.exp(-SPLIT_RATE * SPLIT_RATE * square)
        / square
    )
    stacked = jnp.concatenate([other_charge[None], other_charge[None] * other_pos], axis=0)
    moments = jnp.einsum("...ab,c...b->c...a", factor, stacked, precision=HIGHEST)
    return own_charge * (shifted * moments[0][None] - moments[1:])


def spline(shifted):
    magnitude = jnp.abs(shifted)
    inner = (4.0 - 6.0 * magnitude * magnitude + 3.0 * magnitude * magnitude * magnitude) / 6.0
    outer = (2.0 - magnitude) * (2.0 - magnitude) * (2.0 - magnitude) / 6.0
    return jnp.where(magnitude < 1.0, inner, jnp.where(magnitude < 2.0, outer, 0.0))


def spline_slope(shifted):
    magnitude = jnp.abs(shifted)
    inner = (9.0 * magnitude * magnitude - 12.0 * magnitude) / 6.0
    outer = -(2.0 - magnitude) * (2.0 - magnitude) / 2.0
    return jnp.sign(shifted) * jnp.where(
        magnitude < 1.0, inner, jnp.where(magnitude < 2.0, outer, 0.0)
    )


def spline_tables(fraction):
    offsets = lax.iota(jnp.int32, POINTS + 3).astype(jnp.float32) - 1.0
    shifted = POINTS * fraction[..., None] - offsets
    return (spline(shifted), spline_slope(shifted))


def make_boxes(coords, charged):
    weight_x = spline_tables(coords[0])[0]
    weight_y = spline_tables(coords[1])[0]
    weight_z = spline_tables(coords[2])[0]
    first = (charged[..., None] * weight_x)[..., :, None] * weight_y[..., None, :]
    return jnp.einsum("...aef,...ag->...efg", first, weight_z, precision=HIGHEST)


def placement_table():
    shape = (POINTS + 3, POINTS, 3)
    entry = lax.broadcasted_iota(jnp.int32, shape, 0)
    inside = lax.broadcasted_iota(jnp.int32, shape, 1)
    which = lax.broadcasted_iota(jnp.int32, shape, 2)
    return (entry - 1 == (which - 1) * POINTS + inside).astype(jnp.float32)


def pick_table(cells, length, first, period):
    shape = (cells, POINTS + 3, length)
    cell_idx = lax.broadcasted_iota(jnp.int32, shape, 0)
    entry = lax.broadcasted_iota(jnp.int32, shape, 1)
    point = lax.broadcasted_iota(jnp.int32, shape, 2)
    return (jnp.mod(POINTS * cell_idx + first + entry, period) == point).astype(jnp.float32)


def gauss_matrix(length, width, first_row, rows):
    row_idx = first_row + lax.broadcasted_iota(jnp.int32, (rows, length), 0)
    col_idx = lax.broadcasted_iota(jnp.int32, (rows, length), 1)
    dist = jnp.mod(row_idx - col_idx, length)
    dist = jnp.minimum(dist, length - dist).astype(jnp.float32)
    return jnp.exp(-dist * dist / (2.0 * width * width))


def taps_for(width):
    return [math.exp(-(step * step) / (2.0 * width * width)) for step in range(-REACH, REACH + 1)]


def long_forces(coords, charged, point_box):
    weight_x, slope_x = spline_tables(coords[0])
    weight_y, slope_y = spline_tables(coords[1])
    weight_z, slope_z = spline_tables(coords[2])
    along_z = jnp.einsum("xyzag,xyzefg->xyzaef", weight_z, point_box, precision=HIGHEST)
    sloped_z = jnp.einsum("xyzag,xyzefg->xyzaef", slope_z, point_box, precision=HIGHEST)
    force_x = jnp.einsum("xyzae,xyzaf,xyzaef->xyza", slope_x, weight_y, along_z, precision=HIGHEST)
    force_y = jnp.einsum("xyzae,xyzaf,xyzaef->xyza", weight_x, slope_y, along_z, precision=HIGHEST)
    force_z = jnp.einsum(
        "xyzae,xyzaf,xyzaef->xyza", weight_x, weight_y, sloped_z, precision=HIGHEST
    )
    return -POINTS * charged * jnp.stack([force_x, force_y, force_z])


def short_forces(packed, beside_all):
    extended = jnp.concatenate(
        [beside_all[:, :, :, -1:], beside_all, beside_all[:, :, :, :1]], axis=3
    )

    def add_offset(offset, total):
        start_x = offset // 9
        start_y = offset // 3 % 3
        start_z = offset % 3
        nearby = lax.dynamic_slice(extended, (0, start_x, start_y, start_z, 0), packed.shape)
        offset_vec = jnp.stack([start_x, start_y, start_z]).astype(jnp.float32) - 1.0
        return total + pair_force(packed[:3], packed[3], nearby[:3], nearby[3], offset_vec)

    return lax.fori_loop(0, 27, add_offset, jnp.zeros((3,) + packed.shape[1:], jnp.float32))


def body(positions, charges, counts):
    live_mask = (lax.broadcasted_iota(jnp.int32, charges.shape, 3) < counts[..., None]).astype(
        jnp.float32
    )
    charged = charges * live_mask
    packed = jnp.concatenate([positions, charged[None]], axis=0)
    beside_all = extended_2(packed, (("space", 1), ("sub", 2)), 1)
    brick_x, brick_y, brick_z = (charges.shape[0], charges.shape[1], charges.shape[2])
    short = short_forces(packed, beside_all)
    boxes = make_boxes(beside_all[:3], beside_all[3])
    table = placement_table()
    placed_x = sum(
        (
            jnp.einsum(
                "XYZefg,ej->XYZjfg",
                boxes[2 - which : 2 - which + brick_x],
                table[:, :, which],
                precision=HIGHEST,
            )
            for which in range(3)
        )
    )
    placed_y = sum(
        (
            jnp.einsum(
                "XYZjfg,fl->XYZjlg",
                placed_x[:, 2 - which : 2 - which + brick_y],
                table[:, :, which],
                precision=HIGHEST,
            )
            for which in range(3)
        )
    )
    placed_z = sum(
        (
            jnp.einsum(
                "XYZjlg,gm->XYZjlm",
                jnp.roll(placed_y, which - 1, axis=2),
                table[:, :, which],
                precision=HIGHEST,
            )
            for which in range(3)
        )
    )
    local_x, local_y, local_z = (POINTS * brick_x, POINTS * brick_y, POINTS * brick_z)
    charge_grid = placed_z.transpose(0, 3, 1, 4, 2, 5).reshape(local_x, local_y, local_z)
    margin_grid = extended_2(charge_grid, (("space", 0), ("sub", 1)), REACH + 2)
    rows_x, rows_y = (local_x + 4, local_y + 4)
    fine = jnp.zeros((rows_x, rows_y, local_z), jnp.float32)
    for width, weight in zip(FINE_WIDTHS, FINE_WEIGHTS):
        taps = taps_for(width)
        section = sum(
            (
                taps[step + REACH]
                * lax.slice_in_dim(margin_grid, REACH + step, REACH + step + rows_x, axis=0)
                for step in range(-REACH, REACH + 1)
            )
        )
        section = sum(
            (
                taps[step + REACH]
                * lax.slice_in_dim(section, REACH + step, REACH + step + rows_y, axis=1)
                for step in range(-REACH, REACH + 1)
            )
        )
        section = sum(
            (
                taps[step + REACH] * jnp.roll(section, -step, axis=2)
                for step in range(-REACH, REACH + 1)
            )
        )
        fine = fine + weight * section
    coarse_charge = (
        charge_grid.reshape(local_x // 2, 2, local_y // 2, 2, local_z // 2, 2).sum(axis=(1, 3, 5))
        * 0.125
    )
    coarse_x, coarse_y, coarse_z = (local_x // 2, local_y // 2, local_z // 2)
    total_x = coarse_x * lax.axis_size("space")
    total_y = coarse_y * lax.axis_size("sub")
    first_x = lax.axis_index("space") * coarse_x - 1
    first_y = lax.axis_index("sub") * coarse_y - 1
    matrices_x = [
        gauss_matrix(total_x, total_x / fraction, first_x, coarse_x + 2)
        for fraction in COARSE_FRACTIONS
    ]
    matrices_y = [
        gauss_matrix(total_y, total_y / fraction, first_y, coarse_y + 2)
        for fraction in COARSE_FRACTIONS
    ]
    matrices_z = [
        gauss_matrix(coarse_z, coarse_z / fraction, 0, coarse_z) for fraction in COARSE_FRACTIONS
    ]
    rows_sub = lax.all_gather(coarse_charge, "sub", axis=1, tiled=True)
    whole = lax.all_gather(rows_sub, "space", axis=0, tiled=True)
    contracted = []
    for number in range(2):
        section = jnp.einsum("ri,ijk->rjk", matrices_x[number], whole, precision=HIGHEST)
        contracted.append(jnp.einsum("sj,rjk->rsk", matrices_y[number], section, precision=HIGHEST))
    coarse = jnp.zeros((coarse_x + 2, coarse_y + 2, coarse_z), jnp.float32)
    for number in range(2):
        coarse = coarse + COARSE_WEIGHTS[number] * jnp.einsum(
            "tk,rsk->rst", matrices_z[number], contracted[number], precision=HIGHEST
        )
    lifted = jnp.repeat(jnp.repeat(jnp.repeat(coarse, 2, axis=0), 2, axis=1), 2, axis=2)
    potential = fine + lifted
    pick_x = pick_table(brick_x, rows_x, 1, rows_x)
    pick_y = pick_table(brick_y, rows_y, 1, rows_y)
    pick_z = pick_table(brick_z, local_z, -1, local_z)
    point_box = jnp.einsum("Xei,ijk->Xejk", pick_x, potential, precision=HIGHEST)
    point_box = jnp.einsum("Yfj,Xejk->XYefk", pick_y, point_box, precision=HIGHEST)
    point_box = jnp.einsum("Zgk,XYefk->XYZefg", pick_z, point_box, precision=HIGHEST)
    return short + long_forces(positions, charged, point_box)


def solution(mesh):
    in_specs = (
        P(None, "space", "sub", None, None),
        P("space", "sub", None, None),
        P("space", "sub", None),
    )
    out_specs = P(None, "space", "sub", None, None)
    return jax.shard_map(body, mesh=mesh, in_specs=in_specs, out_specs=out_specs, check_vma=False)
```

profile of v0, /device:TPU:1, one launch (start us, length us, event | category | flops | bytes accessed | tf_op | source)
XLA Modules:
  0.0 296.6 jit_solution(17084310998732448958)
XLA Ops:
  2.3 4.9 %collective-permute-start = (f32[4,1,2,3,128]{4,2,3,1,0:T(2,128)S(1)}, f32[4,1,2,3,128]{4,2,3,1,0:T(2,128)S(1)}, u32[]{:S(2)}, u32[]{:S(2)}) collective-permute-start(f32[4,1,2,3,128]{4,2,3,1,0:T(2,128)S(1)} %get-tuple-element.287), channel_id=1, source_target_pairs={{0,8},{8,16},{16,24},{24,32},{32,40},{40,48},{48,56},{56,64},{64,7... | collective-permute-start | bytes 36872 | tf_op jit(solution)/shard_map/ppermute | solution.py:28
  7.2 5.7 %collective-permute-start.1 = (f32[4,1,2,3,128]{4,2,3,1,0:T(2,128)S(1)}, f32[4,1,2,3,128]{4,2,3,1,0:T(2,128)S(1)}, u32[]{:S(2)}, u32[]{:S(2)}) collective-permute-start(f32[4,1,2,3,128]{4,2,3,1,0:T(2,128)S(1)} %get-tuple-element.288), channel_id=1, source_target_pairs={{8,0},{16,8},{24,16},{32,24},{40,32},{48,40},{56,48},{64,56},{72,6... | collective-permute-start | bytes 36872 | tf_op jit(solution)/shard_map/ppermute | solution.py:29
  14.9 1.9 collective-permute-start.2
  16.8 5.5 %collective-permute-start.3 = (f32[4,4,1,3,128]{4,2,3,1,0:T(1,128)S(1)}, f32[4,4,1,3,128]{4,2,3,1,0:T(1,128)S(1)}, u32[]{:S(2)}, u32[]{:S(2)}) collective-permute-start(f32[4,4,1,3,128]{4,2,3,1,0:T(1,128)S(1)} %get-tuple-element.286), channel_id=1, source_target_pairs={{1,0},{2,1},{3,2},{4,3},{5,4},{6,5},{7,6},{0,7},{9,8},{10,9},{11,1... | collective-permute-start | bytes 73736 | tf_op jit(solution)/shard_map/ppermute | solution.py:29
  24.2 2.6 fusion.85
  30.8 21.9 %all_gather.6 = f32[4,32,6]{2,0,1:T(4,128)S(1)} all-gather(f32[4,4,6]{2,0,1:T(4,128)S(1)} %copy.224), channel_id=1, replica_groups=mesh['space'=64,'sub'=8] {'sub'}, dimensions={1}, use_global_device_ids=true | all-gather | bytes 3456 | tf_op jit(solution)/shard_map/all_gather | solution.py:233
  52.8 89.8 %all_gather.7 = f32[256,32,6]{1,2,0:T(8,128)S(1)} all-gather(f32[4,32,6]{1,2,0:T(8,128)S(1)} %copy.225), channel_id=1, replica_groups=mesh['space'=64,'sub'=8] {'space'}, dimensions={0}, use_global_device_ids=true | all-gather | bytes 199680 | tf_op jit(solution)/shard_map/all_gather | solution.py:234
  144.8 1.9 collective-permute-start.4
  146.7 2.6 collective-permute-start.5
  149.4 130.5 %while.17 = (s32[]{:T(128)}, f32[3,2,2,3,128]{4,0,3,2,1:T(4,128)S(1)}, f32[1,2,2,3,128]{4,3,2,1,0:T(4,128)S(1)}, f32[3,2,2,3,128]{4,0,3,2,1:T(4,128)S(1)}, f32[4...) while((s32[]{:T(128)}, ...), condition=%wide.region_2.3_spmd.clone, body=%wide.region_0.2_spmd.clone.sunk | while | flops 24422448 | bytes 2021951 | solution.py:138
  149.7 0.8 multiply_reduce_fusion.7
  150.6 3.5 %convolution_bitcast_fusion.7 = f32[4,2,2,3,128]{4,0,3,2,1:T(4,128)S(1)} fusion(f32[2,2,3,128,128]{4,3,2,1,0:T(8,128)S(1)} %multiply_reduce_fusion.7, f32[3,2,2,3,128]{4,0,3,2,1:T(4,128)S(1)} %copy_multiply_fusion.2, f32[1,2,2,3,128]{4,0,3,2,1:T(1,128)S(1)} %copy.347), kind=kOutput, calls=%fused_computation.4.clone.1 | convolution fusion | flops 22812672 | bytes 835584 | tf_op jit(solution)/shard_map/while/body/eval_jaxpr/...ab,c...b->c...a/dot_general | solution.py:49
  154.5 0.8 multiply_reduce_fusion.7
  155.5 3.5 %convolution_bitcast_fusion.7 = f32[4,2,2,3,128]{4,0,3,2,1:T(4,128)S(1)} fusion(f32[2,2,3,128,128]{4,3,2,1,0:T(8,128)S(1)} %multiply_reduce_fusion.7, f32[3,2,2,3,128]{4,0,3,2,1:T(4,128)S(1)} %copy_multiply_fusion.2, f32[1,2,2,3,128]{4,0,3,2,1:T(1,128)S(1)} %copy.347), kind=kOutput, calls=%fused_computation.4.clone.1 | convolution fusion | flops 22812672 | bytes 835584 | tf_op jit(solution)/shard_map/while/body/eval_jaxpr/...ab,c...b->c...a/dot_general | solution.py:49
  159.4 0.8 multiply_reduce_fusion.7
  160.3 3.5 %convolution_bitcast_fusion.7 = f32[4,2,2,3,128]{4,0,3,2,1:T(4,128)S(1)} fusion(f32[2,2,3,128,128]{4,3,2,1,0:T(8,128)S(1)} %multiply_reduce_fusion.7, f32[3,2,2,3,128]{4,0,3,2,1:T(4,128)S(1)} %copy_multiply_fusion.2, f32[1,2,2,3,128]{4,0,3,2,1:T(1,128)S(1)} %copy.347), kind=kOutput, calls=%fused_computation.4.clone.1 | convolution fusion | flops 22812672 | bytes 835584 | tf_op jit(solution)/shard_map/while/body/eval_jaxpr/...ab,c...b->c...a/dot_general | solution.py:49
  164.2 0.8 multiply_reduce_fusion.7
  165.1 3.5 %convolution_bitcast_fusion.7 = f32[4,2,2,3,128]{4,0,3,2,1:T(4,128)S(1)} fusion(f32[2,2,3,128,128]{4,3,2,1,0:T(8,128)S(1)} %multiply_reduce_fusion.7, f32[3,2,2,3,128]{4,0,3,2,1:T(4,128)S(1)} %copy_multiply_fusion.2, f32[1,2,2,3,128]{4,0,3,2,1:T(1,128)S(1)} %copy.347), kind=kOutput, calls=%fused_computation.4.clone.1 | convolution fusion | flops 22812672 | bytes 835584 | tf_op jit(solution)/shard_map/while/body/eval_jaxpr/...ab,c...b->c...a/dot_general | solution.py:49
  169.0 0.8 multiply_reduce_fusion.7
  170.0 3.5 %convolution_bitcast_fusion.7 = f32[4,2,2,3,128]{4,0,3,2,1:T(4,128)S(1)} fusion(f32[2,2,3,128,128]{4,3,2,1,0:T(8,128)S(1)} %multiply_reduce_fusion.7, f32[3,2,2,3,128]{4,0,3,2,1:T(4,128)S(1)} %copy_multiply_fusion.2, f32[1,2,2,3,128]{4,0,3,2,1:T(1,128)S(1)} %copy.347), kind=kOutput, calls=%fused_computation.4.clone.1 | convolution fusion | flops 22812672 | bytes 835584 | tf_op jit(solution)/shard_map/while/body/eval_jaxpr/...ab,c...b->c...a/dot_general | solution.py:49
  173.9 0.8 multiply_reduce_fusion.7
  174.8 3.5 %convolution_bitcast_fusion.7 = f32[4,2,2,3,128]{4,0,3,2,1:T(4,128)S(1)} fusion(f32[2,2,3,128,128]{4,3,2,1,0:T(8,128)S(1)} %multiply_reduce_fusion.7, f32[3,2,2,3,128]{4,0,3,2,1:T(4,128)S(1)} %copy_multiply_fusion.2, f32[1,2,2,3,128]{4,0,3,2,1:T(1,128)S(1)} %copy.347), kind=kOutput, calls=%fused_computation.4.clone.1 | convolution fusion | flops 22812672 | bytes 835584 | tf_op jit(solution)/shard_map/while/body/eval_jaxpr/...ab,c...b->c...a/dot_general | solution.py:49
  178.7 0.8 multiply_reduce_fusion.7
  179.6 3.5 %convolution_bitcast_fusion.7 = f32[4,2,2,3,128]{4,0,3,2,1:T(4,128)S(1)} fusion(f32[2,2,3,128,128]{4,3,2,1,0:T(8,128)S(1)} %multiply_reduce_fusion.7, f32[3,2,2,3,128]{4,0,3,2,1:T(4,128)S(1)} %copy_multiply_fusion.2, f32[1,2,2,3,128]{4,0,3,2,1:T(1,128)S(1)} %copy.347), kind=kOutput, calls=%fused_computation.4.clone.1 | convolution fusion | flops 22812672 | bytes 835584 | tf_op jit(solution)/shard_map/while/body/eval_jaxpr/...ab,c...b->c...a/dot_general | solution.py:49
  183.5 0.8 multiply_reduce_fusion.7
  184.5 3.5 %convolution_bitcast_fusion.7 = f32[4,2,2,3,128]{4,0,3,2,1:T(4,128)S(1)} fusion(f32[2,2,3,128,128]{4,3,2,1,0:T(8,128)S(1)} %multiply_reduce_fusion.7, f32[3,2,2,3,128]{4,0,3,2,1:T(4,128)S(1)} %copy_multiply_fusion.2, f32[1,2,2,3,128]{4,0,3,2,1:T(1,128)S(1)} %copy.347), kind=kOutput, calls=%fused_computation.4.clone.1 | convolution fusion | flops 22812672 | bytes 835584 | tf_op jit(solution)/shard_map/while/body/eval_jaxpr/...ab,c...b->c...a/dot_general | solution.py:49
  188.4 0.8 multiply_reduce_fusion.7
  189.3 3.5 %convolution_bitcast_fusion.7 = f32[4,2,2,3,128]{4,0,3,2,1:T(4,128)S(1)} fusion(f32[2,2,3,128,128]{4,3,2,1,0:T(8,128)S(1)} %multiply_reduce_fusion.7, f32[3,2,2,3,128]{4,0,3,2,1:T(4,128)S(1)} %copy_multiply_fusion.2, f32[1,2,2,3,128]{4,0,3,2,1:T(1,128)S(1)} %copy.347), kind=kOutput, calls=%fused_computation.4.clone.1 | convolution fusion | flops 22812672 | bytes 835584 | tf_op jit(solution)/shard_map/while/body/eval_jaxpr/...ab,c...b->c...a/dot_general | solution.py:49
  193.2 0.8 multiply_reduce_fusion.7
  194.1 3.5 %convolution_bitcast_fusion.7 = f32[4,2,2,3,128]{4,0,3,2,1:T(4,128)S(1)} fusion(f32[2,2,3,128,128]{4,3,2,1,0:T(8,128)S(1)} %multiply_reduce_fusion.7, f32[3,2,2,3,128]{4,0,3,2,1:T(4,128)S(1)} %copy_multiply_fusion.2, f32[1,2,2,3,128]{4,0,3,2,1:T(1,128)S(1)} %copy.347), kind=kOutput, calls=%fused_computation.4.clone.1 | convolution fusion | flops 22812672 | bytes 835584 | tf_op jit(solution)/shard_map/while/body/eval_jaxpr/...ab,c...b->c...a/dot_general | solution.py:49
  198.0 0.8 multiply_reduce_fusion.7
  199.0 3.5 %convolution_bitcast_fusion.7 = f32[4,2,2,3,128]{4,0,3,2,1:T(4,128)S(1)} fusion(f32[2,2,3,128,128]{4,3,2,1,0:T(8,128)S(1)} %multiply_reduce_fusion.7, f32[3,2,2,3,128]{4,0,3,2,1:T(4,128)S(1)} %copy_multiply_fusion.2, f32[1,2,2,3,128]{4,0,3,2,1:T(1,128)S(1)} %copy.347), kind=kOutput, calls=%fused_computation.4.clone.1 | convolution fusion | flops 22812672 | bytes 835584 | tf_op jit(solution)/shard_map/while/body/eval_jaxpr/...ab,c...b->c...a/dot_general | solution.py:49
  202.9 0.8 multiply_reduce_fusion.7
  203.8 3.5 %convolution_bitcast_fusion.7 = f32[4,2,2,3,128]{4,0,3,2,1:T(4,128)S(1)} fusion(f32[2,2,3,128,128]{4,3,2,1,0:T(8,128)S(1)} %multiply_reduce_fusion.7, f32[3,2,2,3,128]{4,0,3,2,1:T(4,128)S(1)} %copy_multiply_fusion.2, f32[1,2,2,3,128]{4,0,3,2,1:T(1,128)S(1)} %copy.347), kind=kOutput, calls=%fused_computation.4.clone.1 | convolution fusion | flops 22812672 | bytes 835584 | tf_op jit(solution)/shard_map/while/body/eval_jaxpr/...ab,c...b->c...a/dot_general | solution.py:49
  207.7 0.8 multiply_reduce_fusion.7
  208.6 3.5 %convolution_bitcast_fusion.7 = f32[4,2,2,3,128]{4,0,3,2,1:T(4,128)S(1)} fusion(f32[2,2,3,128,128]{4,3,2,1,0:T(8,128)S(1)} %multiply_reduce_fusion.7, f32[3,2,2,3,128]{4,0,3,2,1:T(4,128)S(1)} %copy_multiply_fusion.2, f32[1,2,2,3,128]{4,0,3,2,1:T(1,128)S(1)} %copy.347), kind=kOutput, calls=%fused_computation.4.clone.1 | convolution fusion | flops 22812672 | bytes 835584 | tf_op jit(solution)/shard_map/while/body/eval_jaxpr/...ab,c...b->c...a/dot_general | solution.py:49
  212.5 0.8 multiply_reduce_fusion.7
  213.5 3.5 %convolution_bitcast_fusion.7 = f32[4,2,2,3,128]{4,0,3,2,1:T(4,128)S(1)} fusion(f32[2,2,3,128,128]{4,3,2,1,0:T(8,128)S(1)} %multiply_reduce_fusion.7, f32[3,2,2,3,128]{4,0,3,2,1:T(4,128)S(1)} %copy_multiply_fusion.2, f32[1,2,2,3,128]{4,0,3,2,1:T(1,128)S(1)} %copy.347), kind=kOutput, calls=%fused_computation.4.clone.1 | convolution fusion | flops 22812672 | bytes 835584 | tf_op jit(solution)/shard_map/while/body/eval_jaxpr/...ab,c...b->c...a/dot_general | solution.py:49
  217.4 0.8 multiply_reduce_fusion.7
  218.3 3.5 %convolution_bitcast_fusion.7 = f32[4,2,2,3,128]{4,0,3,2,1:T(4,128)S(1)} fusion(f32[2,2,3,128,128]{4,3,2,1,0:T(8,128)S(1)} %multiply_reduce_fusion.7, f32[3,2,2,3,128]{4,0,3,2,1:T(4,128)S(1)} %copy_multiply_fusion.2, f32[1,2,2,3,128]{4,0,3,2,1:T(1,128)S(1)} %copy.347), kind=kOutput, calls=%fused_computation.4.clone.1 | convolution fusion | flops 22812672 | bytes 835584 | tf_op jit(solution)/shard_map/while/body/eval_jaxpr/...ab,c...b->c...a/dot_general | solution.py:49
  222.2 0.8 multiply_reduce_fusion.7
  223.1 3.5 %convolution_bitcast_fusion.7 = f32[4,2,2,3,128]{4,0,3,2,1:T(4,128)S(1)} fusion(f32[2,2,3,128,128]{4,3,2,1,0:T(8,128)S(1)} %multiply_reduce_fusion.7, f32[3,2,2,3,128]{4,0,3,2,1:T(4,128)S(1)} %copy_multiply_fusion.2, f32[1,2,2,3,128]{4,0,3,2,1:T(1,128)S(1)} %copy.347), kind=kOutput, calls=%fused_computation.4.clone.1 | convolution fusion | flops 22812672 | bytes 835584 | tf_op jit(solution)/shard_map/while/body/eval_jaxpr/...ab,c...b->c...a/dot_general | solution.py:49
  227.0 0.8 multiply_reduce_fusion.7
  227.9 3.5 %convolution_bitcast_fusion.7 = f32[4,2,2,3,128]{4,0,3,2,1:T(4,128)S(1)} fusion(f32[2,2,3,128,128]{4,3,2,1,0:T(8,128)S(1)} %multiply_reduce_fusion.7, f32[3,2,2,3,128]{4,0,3,2,1:T(4,128)S(1)} %copy_multiply_fusion.2, f32[1,2,2,3,128]{4,0,3,2,1:T(1,128)S(1)} %copy.347), kind=kOutput, calls=%fused_computation.4.clone.1 | convolution fusion | flops 22812672 | bytes 835584 | tf_op jit(solution)/shard_map/while/body/eval_jaxpr/...ab,c...b->c...a/dot_general | solution.py:49
  231.9 0.8 multiply_reduce_fusion.7
  232.8 3.5 %convolution_bitcast_fusion.7 = f32[4,2,2,3,128]{4,0,3,2,1:T(4,128)S(1)} fusion(f32[2,2,3,128,128]{4,3,2,1,0:T(8,128)S(1)} %multiply_reduce_fusion.7, f32[3,2,2,3,128]{4,0,3,2,1:T(4,128)S(1)} %copy_multiply_fusion.2, f32[1,2,2,3,128]{4,0,3,2,1:T(1,128)S(1)} %copy.347), kind=kOutput, calls=%fused_computation.4.clone.1 | convolution fusion | flops 22812672 | bytes 835584 | tf_op jit(solution)/shard_map/while/body/eval_jaxpr/...ab,c...b->c...a/dot_general | solution.py:49
  236.7 0.8 multiply_reduce_fusion.7
  237.6 3.5 %convolution_bitcast_fusion.7 = f32[4,2,2,3,128]{4,0,3,2,1:T(4,128)S(1)} fusion(f32[2,2,3,128,128]{4,3,2,1,0:T(8,128)S(1)} %multiply_reduce_fusion.7, f32[3,2,2,3,128]{4,0,3,2,1:T(4,128)S(1)} %copy_multiply_fusion.2, f32[1,2,2,3,128]{4,0,3,2,1:T(1,128)S(1)} %copy.347), kind=kOutput, calls=%fused_computation.4.clone.1 | convolution fusion | flops 22812672 | bytes 835584 | tf_op jit(solution)/shard_map/while/body/eval_jaxpr/...ab,c...b->c...a/dot_general | solution.py:49
  241.5 0.8 multiply_reduce_fusion.7
  242.4 3.5 %convolution_bitcast_fusion.7 = f32[4,2,2,3,128]{4,0,3,2,1:T(4,128)S(1)} fusion(f32[2,2,3,128,128]{4,3,2,1,0:T(8,128)S(1)} %multiply_reduce_fusion.7, f32[3,2,2,3,128]{4,0,3,2,1:T(4,128)S(1)} %copy_multiply_fusion.2, f32[1,2,2,3,128]{4,0,3,2,1:T(1,128)S(1)} %copy.347), kind=kOutput, calls=%fused_computation.4.clone.1 | convolution fusion | flops 22812672 | bytes 835584 | tf_op jit(solution)/shard_map/while/body/eval_jaxpr/...ab,c...b->c...a/dot_general | solution.py:49
  246.4 0.8 multiply_reduce_fusion.7
  247.3 3.5 %convolution_bitcast_fusion.7 = f32[4,2,2,3,128]{4,0,3,2,1:T(4,128)S(1)} fusion(f32[2,2,3,128,128]{4,3,2,1,0:T(8,128)S(1)} %multiply_reduce_fusion.7, f32[3,2,2,3,128]{4,0,3,2,1:T(4,128)S(1)} %copy_multiply_fusion.2, f32[1,2,2,3,128]{4,0,3,2,1:T(1,128)S(1)} %copy.347), kind=kOutput, calls=%fused_computation.4.clone.1 | convolution fusion | flops 22812672 | bytes 835584 | tf_op jit(solution)/shard_map/while/body/eval_jaxpr/...ab,c...b->c...a/dot_general | solution.py:49
  251.2 0.8 multiply_reduce_fusion.7
  252.1 3.5 %convolution_bitcast_fusion.7 = f32[4,2,2,3,128]{4,0,3,2,1:T(4,128)S(1)} fusion(f32[2,2,3,128,128]{4,3,2,1,0:T(8,128)S(1)} %multiply_reduce_fusion.7, f32[3,2,2,3,128]{4,0,3,2,1:T(4,128)S(1)} %copy_multiply_fusion.2, f32[1,2,2,3,128]{4,0,3,2,1:T(1,128)S(1)} %copy.347), kind=kOutput, calls=%fused_computation.4.clone.1 | convolution fusion | flops 22812672 | bytes 835584 | tf_op jit(solution)/shard_map/while/body/eval_jaxpr/...ab,c...b->c...a/dot_general | solution.py:49
  256.0 0.8 multiply_reduce_fusion.7
  256.9 3.5 %convolution_bitcast_fusion.7 = f32[4,2,2,3,128]{4,0,3,2,1:T(4,128)S(1)} fusion(f32[2,2,3,128,128]{4,3,2,1,0:T(8,128)S(1)} %multiply_reduce_fusion.7, f32[3,2,2,3,128]{4,0,3,2,1:T(4,128)S(1)} %copy_multiply_fusion.2, f32[1,2,2,3,128]{4,0,3,2,1:T(1,128)S(1)} %copy.347), kind=kOutput, calls=%fused_computation.4.clone.1 | convolution fusion | flops 22812672 | bytes 835584 | tf_op jit(solution)/shard_map/while/body/eval_jaxpr/...ab,c...b->c...a/dot_general | solution.py:49
  260.9 0.8 multiply_reduce_fusion.7
  261.8 3.5 %convolution_bitcast_fusion.7 = f32[4,2,2,3,128]{4,0,3,2,1:T(4,128)S(1)} fusion(f32[2,2,3,128,128]{4,3,2,1,0:T(8,128)S(1)} %multiply_reduce_fusion.7, f32[3,2,2,3,128]{4,0,3,2,1:T(4,128)S(1)} %copy_multiply_fusion.2, f32[1,2,2,3,128]{4,0,3,2,1:T(1,128)S(1)} %copy.347), kind=kOutput, calls=%fused_computation.4.clone.1 | convolution fusion | flops 22812672 | bytes 835584 | tf_op jit(solution)/shard_map/while/body/eval_jaxpr/...ab,c...b->c...a/dot_general | solution.py:49
  266.6 3.5 %convolution_bitcast_fusion.7 = f32[4,2,2,3,128]{4,0,3,2,1:T(4,128)S(1)} fusion(f32[2,2,3,128,128]{4,3,2,1,0:T(8,128)S(1)} %multiply_reduce_fusion.7, f32[3,2,2,3,128]{4,0,3,2,1:T(4,128)S(1)} %copy_multiply_fusion.2, f32[1,2,2,3,128]{4,0,3,2,1:T(1,128)S(1)} %copy.347), kind=kOutput, calls=%fused_computation.4.clone.1 | convolution fusion | flops 22812672 | bytes 835584 | tf_op jit(solution)/shard_map/while/body/eval_jaxpr/...ab,c...b->c...a/dot_general | solution.py:49
  271.4 3.5 %convolution_bitcast_fusion.7 = f32[4,2,2,3,128]{4,0,3,2,1:T(4,128)S(1)} fusion(f32[2,2,3,128,128]{4,3,2,1,0:T(8,128)S(1)} %multiply_reduce_fusion.7, f32[3,2,2,3,128]{4,0,3,2,1:T(4,128)S(1)} %copy_multiply_fusion.2, f32[1,2,2,3,128]{4,0,3,2,1:T(1,128)S(1)} %copy.347), kind=kOutput, calls=%fused_computation.4.clone.1 | convolution fusion | flops 22812672 | bytes 835584 | tf_op jit(solution)/shard_map/while/body/eval_jaxpr/...ab,c...b->c...a/dot_general | solution.py:49
  276.3 3.5 %convolution_bitcast_fusion.7 = f32[4,2,2,3,128]{4,0,3,2,1:T(4,128)S(1)} fusion(f32[2,2,3,128,128]{4,3,2,1,0:T(8,128)S(1)} %multiply_reduce_fusion.7, f32[3,2,2,3,128]{4,0,3,2,1:T(4,128)S(1)} %copy_multiply_fusion.2, f32[1,2,2,3,128]{4,0,3,2,1:T(1,128)S(1)} %copy.347), kind=kOutput, calls=%fused_computation.4.clone.1 | convolution fusion | flops 22812672 | bytes 835584 | tf_op jit(solution)/shard_map/while/body/eval_jaxpr/...ab,c...b->c...a/dot_general | solution.py:49
  280.3 3.0 %collective-permute-start.6 = (f32[20,6,12]{1,0,2:T(8,128)S(1)}, f32[20,6,12]{1,0,2:T(8,128)S(1)}, u32[]{:S(2)}, u32[]{:S(2)}) collective-permute-start(f32[20,6,12]{1,0,2:T(8,128)S(1)} %get-tuple-element.239), channel_id=1, source_target_pairs={{0,1},{1,2},{2,3},{3,4},{4,5},{5,6},{6,7},{7,0},{8,9},{9,10},{10,1... | collective-permute-start | bytes 17288 | tf_op jit(solution)/shard_map/ppermute | solution.py:28
  283.3 4.4 %collective-permute-start.7 = (f32[20,6,12]{1,0,2:T(8,128)S(1)}, f32[20,6,12]{1,0,2:T(8,128)S(1)}, u32[]{:S(2)}, u32[]{:S(2)}) collective-permute-start(f32[20,6,12]{1,0,2:T(8,128)S(1)} %get-tuple-element.240), channel_id=1, source_target_pairs={{1,0},{2,1},{3,2},{4,3},{5,4},{6,5},{7,6},{0,7},{9,8},{10,9},{11,1... | collective-permute-start | bytes 17288 | tf_op jit(solution)/shard_map/ppermute | solution.py:29
  288.3 1.9 collective-permute-done.7
  (494 shorter events, 31.7 us)
Async XLA Ops:
  0.0 23.7 %copy-start = (f32[3,2,2,3,128]{4,2,3,1,0:T(2,128)S(1)}, f32[3,2,2,3,128]{4,2,3,1,0:T(2,128)}, u32[]{:S(2)}) copy-start(f32[3,2,2,3,128]{4,2,3,1,0:T(2,128)} %param.5) | copy-start | bytes 55300
  2.3 11.8 %collective-permute-start = (f32[4,1,2,3,128]{4,2,3,1,0:T(2,128)S(1)}, f32[4,1,2,3,128]{4,2,3,1,0:T(2,128)S(1)}, u32[]{:S(2)}, u32[]{:S(2)}) collective-permute-start(f32[4,1,2,3,128]{4,2,3,1,0:T(2,128)S(1)} %get-tuple-element.287), channel_id=1, source_target_pairs={{0,8},{8,16},{16,24},{24,32},{32,40},{40,48},{48,56},{56,64},{64,7... | collective-permute-start | bytes 36872 | tf_op jit(solution)/shard_map/ppermute | solution.py:28
  7.2 6.9 %collective-permute-start.1 = (f32[4,1,2,3,128]{4,2,3,1,0:T(2,128)S(1)}, f32[4,1,2,3,128]{4,2,3,1,0:T(2,128)S(1)}, u32[]{:S(2)}, u32[]{:S(2)}) collective-permute-start(f32[4,1,2,3,128]{4,2,3,1,0:T(2,128)S(1)} %get-tuple-element.288), channel_id=1, source_target_pairs={{8,0},{16,8},{24,16},{32,24},{40,32},{48,40},{56,48},{64,56},{72,6... | collective-permute-start | bytes 36872 | tf_op jit(solution)/shard_map/ppermute | solution.py:29
  14.9 8.8 %collective-permute-start.2 = (f32[4,4,1,3,128]{4,2,3,1,0:T(1,128)S(1)}, f32[4,4,1,3,128]{4,2,3,1,0:T(1,128)S(1)}, u32[]{:S(2)}, u32[]{:S(2)}) collective-permute-start(f32[4,4,1,3,128]{4,2,3,1,0:T(1,128)S(1)} %get-tuple-element.285), channel_id=1, source_target_pairs={{0,1},{1,2},{2,3},{3,4},{4,5},{5,6},{6,7},{7,0},{8,9},{9,10},{10,1... | collective-permute-start | bytes 73736 | tf_op jit(solution)/shard_map/ppermute | solution.py:28
  16.8 6.9 %collective-permute-start.3 = (f32[4,4,1,3,128]{4,2,3,1,0:T(1,128)S(1)}, f32[4,4,1,3,128]{4,2,3,1,0:T(1,128)S(1)}, u32[]{:S(2)}, u32[]{:S(2)}) collective-permute-start(f32[4,4,1,3,128]{4,2,3,1,0:T(1,128)S(1)} %get-tuple-element.286), channel_id=1, source_target_pairs={{1,0},{2,1},{3,2},{4,3},{5,4},{6,5},{7,6},{0,7},{9,8},{10,9},{11,1... | collective-permute-start | bytes 73736 | tf_op jit(solution)/shard_map/ppermute | solution.py:29
  144.8 135.3 %collective-permute-start.4 = (f32[6,8,12]{1,0,2:T(8,128)S(1)}, f32[6,8,12]{1,0,2:T(8,128)S(1)}, u32[]{:S(2)}, u32[]{:S(2)}) collective-permute-start(f32[6,8,12]{1,0,2:T(8,128)S(1)} %get-tuple-element.283), channel_id=1, source_target_pairs={{0,8},{8,16},{16,24},{24,32},{32,40},{40,48},{48,56},{56,64},{64,7... | collective-permute-start | bytes 6920 | tf_op jit(solution)/shard_map/ppermute | solution.py:28
  146.7 133.4 %collective-permute-start.5 = (f32[6,8,12]{1,0,2:T(8,128)S(1)}, f32[6,8,12]{1,0,2:T(8,128)S(1)}, u32[]{:S(2)}, u32[]{:S(2)}) collective-permute-start(f32[6,8,12]{1,0,2:T(8,128)S(1)} %get-tuple-element.284), channel_id=1, source_target_pairs={{8,0},{16,8},{24,16},{32,24},{40,32},{48,40},{56,48},{64,56},{72,6... | collective-permute-start | bytes 6920 | tf_op jit(solution)/shard_map/ppermute | solution.py:29
  280.3 8.0 %collective-permute-start.6 = (f32[20,6,12]{1,0,2:T(8,128)S(1)}, f32[20,6,12]{1,0,2:T(8,128)S(1)}, u32[]{:S(2)}, u32[]{:S(2)}) collective-permute-start(f32[20,6,12]{1,0,2:T(8,128)S(1)} %get-tuple-element.239), channel_id=1, source_target_pairs={{0,1},{1,2},{2,3},{3,4},{4,5},{5,6},{6,7},{7,0},{8,9},{9,10},{10,1... | collective-permute-start | bytes 17288 | tf_op jit(solution)/shard_map/ppermute | solution.py:28
  283.3 6.9 %collective-permute-start.7 = (f32[20,6,12]{1,0,2:T(8,128)S(1)}, f32[20,6,12]{1,0,2:T(8,128)S(1)}, u32[]{:S(2)}, u32[]{:S(2)}) collective-permute-start(f32[20,6,12]{1,0,2:T(8,128)S(1)} %get-tuple-element.240), channel_id=1, source_target_pairs={{1,0},{2,1},{3,2},{4,3},{5,4},{6,5},{7,6},{0,7},{9,8},{10,9},{11,1... | collective-permute-start | bytes 17288 | tf_op jit(solution)/shard_map/ppermute | solution.py:29
where the time goes:
time: 302 us; the launch traced here: 297 us
  blocking collectives  112 us (37%)
  matrix products  103 us (34%)
  other arithmetic  35.6 us (12%)
  starting transfers between devices  30 us (10%)
  local copies, waits for them, and re-layouts  8.59 us (3%)
  loops' own time  5.06 us (2%)
    dot_general x27, matrix products, pair_force(): jnp.einsum('...ab,c...b->c...a', factor, stacked, precision=HIGHEST)  93.2 us
    all_gather x1, blocking collectives, body(): whole = lax.all_gather(rows_sub, 'space', axis=0, tiled=True)  89.8 us
    reduce_sum x27, other arithmetic, pair_force(): square = jnp.sum(spread * spread, axis=0) + SOFT_SQUARE  22.2 us
    all_gather x1, blocking collectives, body(): rows_sub = lax.all_gather(coarse_charge, 'sub', axis=1, tiled=True)  21.9 us
    ppermute x4, starting transfers between devices, extended_2(): after = lax.ppermute(first, axis, down)  18.2 us
    ppermute x4, starting transfers between devices, extended_2(): before = lax.ppermute(last, axis, up)  11.8 us
  transfers between devices with their start and end apart: 8, of which 1 were waited for; matrix products, arithmetic and copies ran while one was open for 43% of the time, Pallas kernels for 0%

commit v1 on v0

v1 whole, which is shorter than its diff:
```python
import functools
import math

import jax
import jax.numpy as jnp
import numpy as np
from jax import lax
from jax.experimental import pallas as pl
from jax.experimental.pallas import tpu as pltpu
from jax.sharding import PartitionSpec as P

F32 = jnp.float32
BF16 = jnp.bfloat16
MESH = pl.DeviceIdType.MESH
HIGHEST = lax.Precision.HIGHEST
SPLIT_RATE = 0.8
SOFT_SQUARE = 0.0625
FINE_WIDTHS = (1.0, 2.0)
FINE_WEIGHTS = (2.0, 0.5)
COARSE_FRACTIONS = (8.0, 4.0)
COARSE_WEIGHTS = (4.0, 2.0)
REACH = 4
SIDES = [(dx, dy) for dx in (-1, 0, 1) for dy in (-1, 0, 1)]
NEAR = [side for side in SIDES if side != (0, 0)]
LAPS = (1, 2, 3, 4, -1, -2, -3, -4)
CELLS = 12


def two_parts(table):
    table = np.asarray(table, np.float32)
    high = table.astype(jnp.bfloat16)
    low = (table - high.astype(np.float32)).astype(jnp.bfloat16)
    return high, low


def constants(sub_size):
    place = np.zeros((4, 2, 64, 128), np.float32)
    for x in range(2):
        for y in range(2):
            for e in range(7):
                for f in range(7):
                    place[2 * x + y, :, 8 * e + f, 11 * (4 * x + e) + 4 * y + f] = 1.0
    place = place.reshape(512, 128).astype(jnp.bfloat16)
    tap = np.arange(11)
    spread = np.zeros((2, 128, 9, 128), np.float32)
    for number, (width, weight) in enumerate(zip(FINE_WIDTHS, FINE_WEIGHTS)):
        for place_num, (dx, dy) in enumerate(SIDES):
            per_axis = []
            for step in (dx, dy):
                dist = np.abs(tap[None, :] + 8 * step - tap[:, None]).astype(np.float64)
                per_axis.append(np.where(dist <= REACH, np.exp(-dist * dist / (2 * width * width)), 0.0))
            both = weight * np.kron(per_axis[0], per_axis[1])
            spread[number, :121, place_num, :121] = both
    spread = two_parts(spread.reshape(256, 9 * 128))
    ring = np.zeros((2, 16, 16), np.float32)
    for number, width in enumerate(FINE_WIDTHS):
        dist = np.abs(np.arange(12)[:, None] - np.arange(12)[None, :])
        dist = np.minimum(dist, 12 - dist).astype(np.float64)
        ring[number, :12, :12] = np.where(dist <= REACH, np.exp(-dist * dist / (2 * width * width)), 0.0)
    ring = ring.reshape(32, 16)
    select = np.zeros((2, 12, 8, 128), np.float32)
    for y in range(2):
        for x in range(11):
            for f in range(7):
                select[y, x, f, 11 * x + 4 * y + f] = 1.0
    select = select.reshape(192, 128).astype(jnp.bfloat16)
    total_y = 4 * sub_size
    coarse = np.zeros((2, 8, 8, sub_size, 16, 8), np.float32)
    for number, (fraction, weight) in enumerate(zip(COARSE_FRACTIONS, COARSE_WEIGHTS)):
        dist = np.abs(np.arange(6)[:, None] - np.arange(6)[None, :])
        dist = np.minimum(dist, 6 - dist).astype(np.float64)
        along_z = np.exp(-dist * dist / (2 * (6 / fraction) ** 2))
        for step in range(sub_size):
            dist = np.mod(4 * step + np.arange(6)[None, :] - np.arange(6)[:, None], total_y)
            dist = np.minimum(dist, total_y - dist).astype(np.float64)
            along_y = np.exp(-dist * dist / (2 * (total_y / fraction) ** 2))
            both = 0.125 * weight * along_z[:, None, :, None] * along_y[None, :, None, :]
            coarse[number, :6, :6, step, :6, :6] = both
    coarse = two_parts(coarse.reshape(128, sub_size * 128))
    return place, spread, ring, select, coarse


def halves(value):
    high = value.astype(BF16).astype(F32)
    return high, value - high


def thirds(value):
    high, rest = halves(value)
    middle, low = halves(rest)
    return high, middle, low


def dot(left, right):
    return lax.dot_general(left, right, (((1,), (0,)), ((), ())), preferred_element_type=F32)


def dot_rows(left, right):
    return lax.dot_general(left, right, (((1,), (1,)), ((), ())), preferred_element_type=F32)


def spline(shifted):
    size = jnp.abs(shifted)
    outer = jnp.maximum(2.0 - size, 0.0)
    inner = jnp.maximum(1.0 - size, 0.0)
    return outer * outer * outer * (1.0 / 6.0) - inner * inner * inner * (2.0 / 3.0)


def spline_slope(shifted):
    size = jnp.abs(shifted)
    outer = jnp.maximum(2.0 - size, 0.0)
    inner = jnp.maximum(1.0 - size, 0.0)
    slope = 2.0 * inner * inner - 0.5 * outer * outer
    return jnp.where(shifted < 0.0, -slope, slope)


def wrapped(shifted):
    return jnp.where(shifted > 6.0, shifted - 12.0, jnp.where(shifted < -6.0, shifted + 12.0, shifted))


def row_iota(rows, lanes=128):
    return lax.broadcasted_iota(jnp.int32, (rows, lanes), 0)


def kernel(
    spaces, subs,
    pos_ref, charge_ref, count_ref, place_hbm, wide_hi_hbm, wide_lo_hbm, ring_ref, select_hbm, far_hi_hbm, far_lo_hbm,
    out_ref,
    place_ref, wide_hi, wide_lo, select_ref, far_hi, far_lo,
    ext, lap_buf, plane_out, plane_buf, fine_out, fine_buf,
    fine_sum, by_ref, wz_ref, pair_hi, pair_lo, vx_ref, left_ref, right_ref, mom_ref, force_ref,
    const_sem, halo_send, halo_recv, lap_send, lap_recv, relay_send, relay_recv, fine_send, fine_recv, plane_send, plane_recv,
):
    laps = spaces // 4
    space = lax.axis_index("space")
    sub = lax.axis_index("sub")
    outer_x = space // (2 * laps)
    lap = (space // 2) % laps
    core = space % 2

    loads = [
        pltpu.make_async_copy(src, dst, const_sem.at[num])
        for num, (src, dst) in enumerate((
            (place_hbm, place_ref), (wide_hi_hbm, wide_hi), (wide_lo_hbm, wide_lo),
            (select_hbm, select_ref), (far_hi_hbm, far_hi), (far_lo_hbm, far_lo),
        ))
    ]
    for load in loads:
        load.start()

    def near_id(side):
        return {"space": (space + side[0] + spaces) % spaces, "sub": (sub + side[1] + subs) % subs}

    def lap_id(step):
        return {"space": outer_x * 2 * laps + ((lap + step + laps) % laps) * 2 + core, "sub": sub}

    def plane_id(member, step):
        return {
            "space": ((outer_x + member // 2) % 2) * 2 * laps + lap * 2 + (core + member % 2) % 2,
            "sub": (sub + step) % subs,
        }

    members = [(member, step) for member in range(4) for step in range(subs) if (member, step) != (0, 0)]
    barrier = pltpu.get_barrier_semaphore()
    for side in NEAR:
        pl.semaphore_signal(barrier, inc=1, device_id=near_id(side), device_id_type=MESH)
    for step in LAPS:
        pl.semaphore_signal(barrier, inc=1, device_id=lap_id(step), device_id_type=MESH)
    for member, step in members:
        pl.semaphore_signal(barrier, inc=1, device_id=plane_id(member, step), device_id_type=MESH)

    lane = lax.broadcasted_iota(jnp.int32, (1, 128), 1)
    for x in range(2):
        for y in range(2):
            for z in range(3):
                lanes = pl.ds(128 * z, 128)
                for k in range(3):
                    ext[1 + x, 1 + y, pl.ds(k, 1), lanes] = pos_ref[k, x, y, pl.ds(z, 1), :]
                live = lane < count_ref[x, y, z]
                ext[1 + x, 1 + y, pl.ds(3, 1), lanes] = jnp.where(live, charge_ref[x, y, pl.ds(z, 1), :], 0.0)
            ext[1 + x, 1 + y, pl.ds(4, 4), :] = jnp.zeros((4, 384), F32)

    def cell_rows(cell):
        x, y, z = cell // 6, (cell // 3) % 2, cell % 3
        block = ext[1 + x, 1 + y, :, pl.ds(pl.multiple_of(z * 128, 128), 128)]
        return x, y, z, block

    row8 = row_iota(8).astype(F32)
    row16 = row_iota(16).astype(F32)

    def coarse_step(cell, total):
        x, y, z, block = cell_rows(cell)
        at_x = 4.0 * block[0:1] + (4 * x + 2).astype(F32) - 2.0 * row8
        at_y = 4.0 * block[1:2] + (4 * y + 2).astype(F32) - 2.0 * row8
        at_z = 4.0 * block[2:3] + (4 * z).astype(F32) - 2.0 * row8
        charge = block[3:4]
        near_z, next_z = wrapped(at_z), wrapped(at_z - 1.0)
        some = row8 < 6.0
        vx = spline(at_x) + spline(at_x - 1.0)
        vy = spline(at_y) + spline(at_y - 1.0)
        vz = jnp.where(some, spline(near_z) + spline(next_z), 0.0)
        sx = spline_slope(at_x) + spline_slope(at_x - 1.0)
        sy = spline_slope(at_y) + spline_slope(at_y - 1.0)
        sz = jnp.where(some, spline_slope(near_z) + spline_slope(next_z), 0.0)
        vz_charge = vz * charge
        pad = jnp.zeros((16, 128), F32)
        product = jnp.concatenate([vz_charge[k : k + 1] * vy for k in range(6)], axis=0)
        high, low = halves(product)
        right = jnp.concatenate([high, pad, high, pad, low, pad, low, pad], axis=0).astype(BF16)
        left = jnp.concatenate(halves(vx), axis=0).astype(BF16)
        lanes = pl.ds(pl.multiple_of(cell * 384, 128), 384)
        tables = jnp.concatenate(
            [
                jnp.concatenate([one[k : k + 1] * other for k in range(6)], axis=0)
                for one, other in ((vz, vy), (vz, sy), (sz, vy))
            ],
            axis=1,
        )
        high, low = halves(tables)
        pair_hi[:, lanes] = high.astype(BF16)
        pair_lo[:, lanes] = low.astype(BF16)
        vx_ref[:, lanes] = jnp.concatenate([sx, vx, vx], axis=1)
        return total + dot_rows(left, right)

    total = lax.fori_loop(0, CELLS, coarse_step, jnp.zeros((16, 256), F32))
    total = total[0:8] + total[8:16]
    lap_buf[0] = total[:, 0:128] + total[:, 128:256]

    pl.semaphore_wait(barrier, len(NEAR) + len(LAPS) + len(members))

    lap_copies = []
    for num, step in enumerate(LAPS):
        copy = pltpu.make_async_remote_copy(
            src_ref=lap_buf.at[0], dst_ref=lap_buf.at[(-step) % laps], send_sem=lap_send.at[num], recv_sem=lap_recv.at[num],
            device_id=lap_id(step), device_id_type=MESH,
        )
        copy.start()
        lap_copies.append(copy)

    def piece(step, far):
        if step == 0:
            return pl.ds(1, 2)
        if far:
            return pl.ds(0 if step > 0 else 3, 1)
        return pl.ds(2 if step > 0 else 1, 1)

    halo_copies = []
    for num, side in enumerate(NEAR):
        copy = pltpu.make_async_remote_copy(
            src_ref=ext.at[piece(side[0], False), piece(side[1], False)],
            dst_ref=ext.at[piece(side[0], True), piece(side[1], True)],
            send_sem=halo_send.at[num], recv_sem=halo_recv.at[num], device_id=near_id(side), device_id_type=MESH,
        )
        copy.start()
        halo_copies.append(copy)

    fine_sum[...] = jnp.zeros_like(fine_sum)

    def fine_step(cell, carry):
        x, y, z, block = cell_rows(cell)
        at_x = 4.0 * block[0:1] - (row8 - 1.0)
        at_y = 4.0 * block[1:2] - (row8 - 1.0)
        at_z = wrapped(4.0 * block[2:3] + (4 * z).astype(F32) - row16)
        bx, by = spline(at_x), spline(at_y)
        bz = jnp.where(row16 < 12.0, spline(at_z), 0.0)
        sz = jnp.where(row16 < 12.0, spline_slope(at_z), 0.0)
        by_ref[cell] = jnp.concatenate([bx, spline_slope(at_x), by, spline_slope(at_y)], axis=0)
        bx_charge = bx * block[3:4]
        product = jnp.concatenate([bx_charge[e : e + 1] * by for e in range(7)] + [jnp.zeros((8, 128), F32)], axis=0)
        right = jnp.concatenate(halves(product), axis=0).astype(BF16)
        high, low = halves(jnp.concatenate([bz, sz], axis=1))
        left = jnp.concatenate([high[:, 0:128], low[:, 0:128]], axis=0).astype(BF16)
        wz_ref[cell] = jnp.concatenate([high, high, high, low, low, low], axis=0).astype(BF16)
        fine_sum[cell // 3] += dot_rows(left, right)
        return carry

    lax.fori_loop(0, CELLS, fine_step, 0)
    for load in loads:
        load.wait()
    boxes = jnp.concatenate([fine_sum[num, 0:16] + fine_sum[num, 16:32] for num in range(4)], axis=1)
    spots = dot(jnp.concatenate(thirds(boxes), axis=0).astype(BF16), place_ref[...])
    spots = spots[0:16] + spots[16:32] + spots[32:48]
    rings = lax.dot_general(
        ring_ref[...], spots, (((1,), (0,)), ((), ())), precision=HIGHEST, preferred_element_type=F32
    )
    rings = jnp.concatenate([rings[0:16], rings[16:32]], axis=1)
    parts = jnp.concatenate(halves(rings), axis=0).astype(BF16)
    fine_all = dot(parts, wide_hi[...])
    fine_all = fine_all[0:16] + fine_all[16:32] + dot(parts[0:16], wide_lo[...])
    for num in range(9):
        fine_out[num] = fine_all[:, 128 * num : 128 * (num + 1)]
    fine_copies = []
    for num, side in enumerate(NEAR):
        copy = pltpu.make_async_remote_copy(
            src_ref=fine_out.at[SIDES.index(side)], dst_ref=fine_buf.at[num],
            send_sem=fine_send.at[num], recv_sem=fine_recv.at[num], device_id=near_id(side), device_id_type=MESH,
        )
        copy.start()
        fine_copies.append(copy)

    for copy in lap_copies:
        copy.wait_recv()
    relays = []
    for num, (src, dst, step) in enumerate((
        (pl.ds(1, 4), pl.ds(5, 4), -4),
        (pl.ds(laps - 3, 3), pl.ds(laps - 7, 3), 4),
    )):
        copy = pltpu.make_async_remote_copy(
            src_ref=lap_buf.at[src], dst_ref=lap_buf.at[dst], send_sem=relay_send.at[num], recv_sem=relay_recv.at[num],
            device_id=lap_id(step), device_id_type=MESH,
        )
        copy.start()
        relays.append(copy)

    for copy in halo_copies:
        copy.wait_recv()

    row_w = row_iota(8, 640)
    slot_w = lax.broadcasted_iota(jnp.int32, (8, 640), 1) // 128

    def column_step(column, carry):
        x, y = column // 4, column % 4
        block = ext[x, y]
        block = jnp.concatenate([block[:, 256:384], block, block[:, 0:128]], axis=1)
        shift = jnp.where(
            row_w == 0, (x - 2).astype(F32), jnp.where(row_w == 1, (y - 2).astype(F32), slot_w.astype(F32) - 2.5)
        )
        coords = jnp.where(row_w < 3, SPLIT_RATE * (block + shift), 0.0)
        square = jnp.sum(coords * coords, axis=0, keepdims=True) + SPLIT_RATE * SPLIT_RATE * SOFT_SQUARE
        ones = jnp.where(row_w == 3, 1.0, 0.0)
        p1, p2, p3 = thirds(coords)
        s1, s2, s3 = thirds(square)

        def with_square(part, square_part):
            return jnp.where(row_w == 4, square_part, part + ones)

        right_ref[column] = jnp.concatenate(
            [with_square(p1, s1), with_square(p2, s2), with_square(p1, s3), p3, p2, p1], axis=0
        ).astype(BF16)
        moments = (coords + ones) * block[3:4]
        m1, m2, m3 = thirds(moments)
        mom_ref[column] = jnp.concatenate([m1, m2, m3, jnp.zeros_like(m1)], axis=0).astype(BF16)
        return carry

    lax.fori_loop(0, 16, column_step, 0)

    row_c = row_iota(8)

    def left_step(cell, carry):
        x, y, z, block = cell_rows(cell)
        shift = jnp.where(
            row_c == 0, (x - 1).astype(F32), jnp.where(row_c == 1, (y - 1).astype(F32), z.astype(F32) - 1.5)
        )
        coords = jnp.where(row_c < 3, SPLIT_RATE * (block + shift), 0.0)
        square = jnp.sum(coords * coords, axis=0, keepdims=True)
        ones = jnp.where(row_c == 4, 1.0, 0.0)
        p1, p2, p3 = thirds(-2.0 * coords)
        s1, s2, s3 = thirds(square)

        def with_square(part, square_part):
            return jnp.where(row_c == 3, square_part, part + ones)

        stacked = jnp.concatenate(
            [with_square(p1, s1), with_square(p1, s2), with_square(p2, s3), p1, p2, p3, jnp.zeros((80, 128), F32)], axis=0
        )
        left_ref[cell] = jnp.transpose(stacked).astype(BF16)
        return carry

    lax.fori_loop(0, CELLS, left_step, 0)

    def pair_step(cell, carry):
        x, y, z, block = cell_rows(cell)
        left = left_ref[cell][:, 0:48]

        def column_pairs(side, moments):
            column = (x + side // 3) * 4 + y + side % 3
            for slot in range(3):
                lanes = pl.ds(pl.multiple_of((z + slot) * 128, 128), 128)
                square = dot(left, right_ref[column, :, lanes])
                inverse = lax.rsqrt(square)
                far = 1.0 - lax.erf(square * inverse)
                bell = jnp.exp2(square * (-math.log2(math.e)))
                factor = (inverse * inverse) * (far * inverse + (2.0 / math.sqrt(math.pi)) * bell)
                high = factor.astype(BF16)
                low = (factor - high.astype(F32)).astype(BF16)
                other = mom_ref[column, :, lanes]
                moments = moments + dot_rows(
                    jnp.concatenate([high, low], axis=1), jnp.concatenate([other, other], axis=1)
                )
            return moments

        moments = lax.fori_loop(0, 9, column_pairs, jnp.zeros((128, 32), F32))
        moments = jnp.transpose(moments)
        moments = moments[0:8] + moments[8:16] + moments[16:24]
        shift = jnp.where(
            row_c == 0, (x - 1).astype(F32), jnp.where(row_c == 1, (y - 1).astype(F32), z.astype(F32) - 1.5)
        )
        coords = SPLIT_RATE * (block + shift)
        force_ref[cell] = (SPLIT_RATE * SPLIT_RATE) * block[3:4] * (coords * moments[3:4] - moments)
        return carry

    lax.fori_loop(0, 4, pair_step, 0)

    for copy in relays:
        copy.wait_recv()
    rows = lax.broadcasted_iota(jnp.int32, (64, 128), 0)
    cols = lax.broadcasted_iota(jnp.int32, (64, 128), 1)
    member = (rows // 8) % 4
    to_space = ((outer_x + member // 2) % 2) * 2 * laps + lap * 2 + (core + member % 2) % 2
    from_space = outer_x * 2 * laps + ((lap + cols // 8) % laps) * 2 + core
    total_x = 4 * spaces
    dist = (4 * (to_space - from_space) + rows % 8 - cols % 8 + 2 * total_x) % total_x
    dist = jnp.minimum(dist, total_x - dist).astype(F32)
    wide = [2.0 * (total_x / fraction) ** 2 for fraction in COARSE_FRACTIONS]
    bells = jnp.exp(-dist * dist * jnp.where(rows < 32, 1.0 / wide[0], 1.0 / wide[1]))
    gathered = jnp.concatenate([lap_buf[num] for num in range(laps)], axis=0)
    along_x = lax.dot_general(
        bells, gathered, (((1,), (0,)), ((), ())), precision=HIGHEST, preferred_element_type=F32
    )
    along_x = jnp.where(lax.broadcasted_iota(jnp.int32, (32, 128), 1) < 64, along_x[0:32], along_x[32:64])
    parts = jnp.concatenate(halves(along_x), axis=0).astype(BF16)
    shares = dot(parts, far_hi[...])
    shares = shares[0:32] + shares[32:64] + dot(parts[0:32], far_lo[...])
    for member_num in range(4):
        for step in range(subs):
            plane_out[member_num * subs + step] = shares[8 * member_num : 8 * member_num + 8, 128 * step : 128 * (step + 1)]
    plane_copies = []
    for member_num, step in members:
        num = member_num * subs + step
        copy = pltpu.make_async_remote_copy(
            src_ref=plane_out.at[num], dst_ref=plane_buf.at[num], send_sem=plane_send.at[num], recv_sem=plane_recv.at[num],
            device_id=plane_id(member_num, step), device_id_type=MESH,
        )
        copy.start()
        plane_copies.append(copy)

    lax.fori_loop(4, CELLS, pair_step, 0)

    for copy in fine_copies:
        copy.wait_recv()
    fine = fine_out[SIDES.index((0, 0))]
    for num in range(8):
        fine = fine + fine_buf[num]
    pieces = thirds(fine)
    points = dot_rows(select_ref[...], jnp.concatenate(pieces + pieces, axis=0).astype(BF16)).astype(BF16)
    fine_sum_rows = points

    def interpolate(cell, x, y):
        start = 96 * y + 32 * x
        spread = dot(fine_sum_rows[start : start + 64], wz_ref[cell])
        tables = by_ref[cell]
        u1 = jnp.zeros((8, 128), F32)
        u2 = jnp.zeros((8, 128), F32)
        u3 = jnp.zeros((8, 128), F32)
        for e in range(7):
            at = spread[8 * e : 8 * e + 8]
            u1 = u1 + tables[8 + e : 9 + e] * at[:, 0:128]
            u2 = u2 + tables[e : e + 1] * at[:, 0:128]
            u3 = u3 + tables[e : e + 1] * at[:, 128:256]
        by, sy = tables[16:24], tables[24:32]
        return [jnp.sum(one * other, axis=0, keepdims=True) for one, other in ((by, u1), (sy, u2), (by, u3))]

    fine_forces = [interpolate(cell, cell // 6, (cell // 3) % 2) for cell in range(CELLS)]

    for copy in plane_copies:
        copy.wait_recv()
    window = plane_out[0]
    for member_num, step in members:
        window = window + plane_buf[member_num * subs + step]
    parts = jnp.concatenate(halves(window), axis=0).astype(BF16)[:, 0:48]
    for cell in range(CELLS):
        x, y, z = cell // 6, (cell // 3) % 2, cell % 3
        lanes = pl.ds(384 * cell, 384)
        spread = dot(parts, pair_hi[:, lanes])
        spread = spread[0:8] + spread[8:16] + dot(parts, pair_lo[:, lanes])[0:8]
        spread = jnp.sum(spread * vx_ref[:, lanes], axis=0, keepdims=True)
        charge = ext[1 + x, 1 + y, pl.ds(3, 1), pl.ds(128 * z, 128)]
        for k in range(3):
            far = fine_forces[cell][k] + spread[:, 128 * k : 128 * (k + 1)]
            out_ref[k, x, y, pl.ds(z, 1), :] = force_ref[cell, pl.ds(k, 1), :] - 4.0 * charge * far

    for copy in lap_copies + halo_copies + fine_copies + relays + plane_copies:
        copy.wait_send()


def solution(mesh):
    spaces, subs = mesh.shape["space"], mesh.shape["sub"]
    laps = spaces // 4
    place, spread, ring, select, coarse = constants(subs)

    def body(positions, charges, counts):
        any_spec = pl.BlockSpec(memory_space=pl.ANY)
        vmem_spec = pl.BlockSpec(memory_space=pltpu.VMEM)
        planes = 4 * subs
        return pl.pallas_call(
            functools.partial(kernel, spaces, subs),
            out_shape=jax.ShapeDtypeStruct(positions.shape, F32),
            in_specs=[vmem_spec, vmem_spec, pl.BlockSpec(memory_space=pltpu.SMEM), any_spec, any_spec, any_spec, vmem_spec, any_spec, any_spec, any_spec],
            out_specs=vmem_spec,
            scratch_shapes=[
                pltpu.VMEM((512, 128), BF16),
                pltpu.VMEM((256, 1152), BF16),
                pltpu.VMEM((256, 1152), BF16),
                pltpu.VMEM((192, 128), BF16),
                pltpu.VMEM((128, 128 * subs), BF16),
                pltpu.VMEM((128, 128 * subs), BF16),
                pltpu.VMEM((4, 4, 8, 384), F32),
                pltpu.VMEM((laps, 8, 128), F32),
                pltpu.VMEM((planes, 8, 128), F32),
                pltpu.VMEM((planes, 8, 128), F32),
                pltpu.VMEM((9, 16, 128), F32),
                pltpu.VMEM((8, 16, 128), F32),
                pltpu.VMEM((4, 32, 128), F32),
                pltpu.VMEM((CELLS, 32, 128), F32),
                pltpu.VMEM((CELLS, 96, 256), BF16),
                pltpu.VMEM((48, CELLS * 384), BF16),
                pltpu.VMEM((48, CELLS * 384), BF16),
                pltpu.VMEM((8, CELLS * 384), F32),
                pltpu.VMEM((CELLS, 128, 128), BF16),
                pltpu.VMEM((16, 48, 640), BF16),
                pltpu.VMEM((16, 32, 640), BF16),
                pltpu.VMEM((CELLS, 8, 128), F32),
                pltpu.SemaphoreType.DMA((6,)),
                pltpu.SemaphoreType.DMA((8,)),
                pltpu.SemaphoreType.DMA((8,)),
                pltpu.SemaphoreType.DMA((8,)),
                pltpu.SemaphoreType.DMA((8,)),
                pltpu.SemaphoreType.DMA((2,)),
                pltpu.SemaphoreType.DMA((2,)),
                pltpu.SemaphoreType.DMA((8,)),
                pltpu.SemaphoreType.DMA((8,)),
                pltpu.SemaphoreType.DMA((planes,)),
                pltpu.SemaphoreType.DMA((planes,)),
            ],
            compiler_params=pltpu.CompilerParams(collective_id=0, has_side_effects=True),
        )(
            positions, charges, counts,
            jnp.asarray(place), jnp.asarray(spread[0]), jnp.asarray(spread[1]), jnp.asarray(ring), jnp.asarray(select),
            jnp.asarray(coarse[0]), jnp.asarray(coarse[1]),
        )

    in_specs = (
        P(None, "space", "sub", None, None),
        P("space", "sub", None, None),
        P("space", "sub", None),
    )
    out_specs = P(None, "space", "sub", None, None)
    return jax.shard_map(body, mesh=mesh, in_specs=in_specs, out_specs=out_specs, check_vma=False)
```

time: 302 us -> 85.8 us (0.28); the launches traced: 297 us -> 85.5 us
  blocking collectives: 112 us -> 0 us
  matrix products: 103 us -> 0 us
  Pallas kernels: 0 us -> 81.5 us
  other arithmetic: 35.6 us -> 0 us
  starting transfers between devices: 30 us -> 0 us
  loops' own time: 5.06 us -> 0 us
  local copies, waits for them, and re-layouts: 8.59 us -> 3.97 us
    all_gather x2 -> x0, blocking collectives: 112 us -> none  [the longest x1 89.8 us: body(): whole = lax.all_gather(rows_sub, 'space', axis=0, tiled=True)]
    dot_general x48 -> x0, matrix products: 103 us -> none  [the longest x27 93.2 us: pair_force(): jnp.einsum('...ab,c...b->c...a', factor, stacked, precision=HIGHEST)]
    pallas_call x0 -> x1, Pallas kernels: none -> 81.5 us  [body(): pl.pallas_call(functools.partial(kernel, spaces, subs), out_shape=jax.Sha...]
    ppermute x8 -> x0, starting transfers between devices: 30 us -> none  [the longest x4 18.2 us: extended_2(): after = lax.ppermute(first, axis, down)]
    reduce_sum x28 -> x0, other arithmetic: 22.3 us -> none  [the longest x27 22.2 us: pair_force(): square = jnp.sum(spread * spread, axis=0) + SOFT_SQUARE]
    another operation x1 -> x0, loops' own time: 5.06 us -> none  [short_forces(): lax.fori_loop(0, 27, add_offset, jnp.zeros((3,) + packed.shape[1:], jnp.f...]
    sub x56 -> x0, other arithmetic: 4.19 us -> none  [the longest x27 2.12 us: add_offset(): jnp.stack([start_x, start_y, start_z]).astype(jnp.float32) - 1.0]
    add x35 -> x0, other arithmetic: 4 us -> none  [the longest x27 2.47 us: add_offset(): total + pair_force(packed[:3], packed[3], nearby[:3], nearby[3], offset_vec)]
  transfers between devices with their start and end apart: 8 -> 0, of which waited for: 1 -> 0; matrix products, arithmetic and copies ran while one was open for 43% -> 0% of each run, Pallas kernels for 0% -> 0%
where the time goes in v1:
time: 85.8 us; the launch traced here: 85.5 us
  Pallas kernels  81.5 us (95%)
  local copies, waits for them, and re-layouts  3.97 us (5%)
    pallas_call x1, Pallas kernels, body(): pl.pallas_call(functools.partial(kernel, spaces, subs), out_shape=jax.Sha...  81.5 us
    unnamed x2, local copies, waits for them, and re-layouts  2.61 us

profile of v1, /device:TPU:1, one launch (start us, length us, event | category | flops | bytes accessed | tf_op | source)
XLA Modules:
  0.0 85.5 jit_solution(16033813312459121287)
XLA Ops:
  0.0 1.3 %copy.12.charge_ref = f32[2,2,3,128]{3,2,1,0:T(4,128)} copy(f32[2,2,3,128]{3,1,2,0:T(2,128)} %param.11) | data formatting | bytes 12288 | tf_op args[1]
  1.3 1.3 %copy.11.pos_ref = f32[3,2,2,3,128]{4,3,2,1,0:T(4,128)} copy(f32[3,2,2,3,128]{4,2,3,1,0:T(2,128)} %param.10) | data formatting | bytes 36864 | tf_op args[0]
  2.6 81.5 %shard_map.100 = f32[3,2,2,3,128]{4,3,2,1,0:T(4,128)} custom-call(f32[3,2,2,3,128]{4,3,2,1,0:T(4,128)} %copy.11.pos_ref, f32[2,2,3,128]{3,2,1,0:T(4,128)} %copy.12.charge_ref, s32[2,2,3]{2,1,0:T(2,128)} %count_ref.1, bf16[512,128]{1,0:T(8,128)(2,1)} %constant.14.clone.place_hbm, bf16[256,1152]{1,0:T(8,128)(2,1)} %constant.15.clone.wide_hi_hbm, ...), custom_call_target="tpu_custom_call" | custom-call | tf_op jit(solution)/shard_map/pallas_call | solution.py:495
  84.1 1.4 %copy.13 = f32[3,2,2,3,128]{4,2,3,1,0:T(2,128)} copy(f32[3,2,2,3,128]{4,3,2,1,0:T(4,128)} %shard_map.100) | data formatting | bytes 36864 | tf_op jit(solution)/shard_map/pallas_call | solution.py:495

commit v2 on v1

--- a/solution.py
+++ b/solution.py
@@ -118,6 +118,15 @@
     return jnp.where(shifted > 6.0, shifted - 12.0, jnp.where(shifted < -6.0, shifted + 12.0, shifted))
 
 
+def grouped(size, step, start, cells=CELLS):
+    def group(number, carry):
+        for num in range(size):
+            carry = step(number * size + num, carry)
+        return carry
+
+    return lax.fori_loop(0, cells // size, group, start)
+
+
 def row_iota(rows, lanes=128):
     return lax.broadcasted_iota(jnp.int32, (rows, lanes), 0)
 
@@ -175,9 +184,9 @@
             for z in range(3):
                 lanes = pl.ds(128 * z, 128)
                 for k in range(3):
-                    ext[1 + x, 1 + y, pl.ds(k, 1), lanes] = pos_ref[k, x, y, pl.ds(z, 1), :]
+                    ext[1 + x, 1 + y, pl.ds(k, 1), lanes] = pos_ref[k, x, z, pl.ds(y, 1), :]
                 live = lane < count_ref[x, y, z]
-                ext[1 + x, 1 + y, pl.ds(3, 1), lanes] = jnp.where(live, charge_ref[x, y, pl.ds(z, 1), :], 0.0)
+                ext[1 + x, 1 + y, pl.ds(3, 1), lanes] = jnp.where(live, charge_ref[x, z, pl.ds(y, 1), :], 0.0)
             ext[1 + x, 1 + y, pl.ds(4, 4), :] = jnp.zeros((4, 384), F32)
 
     def cell_rows(cell):
@@ -222,7 +231,7 @@
         vx_ref[:, lanes] = jnp.concatenate([sx, vx, vx], axis=1)
         return total + dot_rows(left, right)
 
-    total = lax.fori_loop(0, CELLS, coarse_step, jnp.zeros((16, 256), F32))
+    total = grouped(6, coarse_step, jnp.zeros((16, 256), F32))
     total = total[0:8] + total[8:16]
     lap_buf[0] = total[:, 0:128] + total[:, 128:256]
 
@@ -274,7 +283,7 @@
         fine_sum[cell // 3] += dot_rows(left, right)
         return carry
 
-    lax.fori_loop(0, CELLS, fine_step, 0)
+    grouped(6, fine_step, 0)
     for load in loads:
         load.wait()
     boxes = jnp.concatenate([fine_sum[num, 0:16] + fine_sum[num, 16:32] for num in range(4)], axis=1)
@@ -366,30 +375,25 @@
         left_ref[cell] = jnp.transpose(stacked).astype(BF16)
         return carry
 
-    lax.fori_loop(0, CELLS, left_step, 0)
+    grouped(6, left_step, 0)
 
     def pair_step(cell, carry):
         x, y, z, block = cell_rows(cell)
         left = left_ref[cell][:, 0:48]
 
-        def column_pairs(side, moments):
+        moments = jnp.zeros((128, 32), F32)
+        lanes = pl.ds(pl.multiple_of(z * 128, 128), 384)
+        for side in range(9):
             column = (x + side // 3) * 4 + y + side % 3
-            for slot in range(3):
-                lanes = pl.ds(pl.multiple_of((z + slot) * 128, 128), 128)
-                square = dot(left, right_ref[column, :, lanes])
-                inverse = lax.rsqrt(square)
-                far = 1.0 - lax.erf(square * inverse)
-                bell = jnp.exp2(square * (-math.log2(math.e)))
-                factor = (inverse * inverse) * (far * inverse + (2.0 / math.sqrt(math.pi)) * bell)
-                high = factor.astype(BF16)
-                low = (factor - high.astype(F32)).astype(BF16)
-                other = mom_ref[column, :, lanes]
-                moments = moments + dot_rows(
-                    jnp.concatenate([high, low], axis=1), jnp.concatenate([other, other], axis=1)
-                )
-            return moments
-
-        moments = lax.fori_loop(0, 9, column_pairs, jnp.zeros((128, 32), F32))
+            square = dot(left, right_ref[column, :, lanes])
+            inverse = lax.rsqrt(square)
+            far = 1.0 - lax.erf(square * inverse)
+            bell = jnp.exp2(square * (-math.log2(math.e)))
+            factor = (inverse * inverse) * (far * inverse + (2.0 / math.sqrt(math.pi)) * bell)
+            high = factor.astype(BF16)
+            low = (factor - high.astype(F32)).astype(BF16)
+            other = mom_ref[column, :, lanes]
+            moments = moments + dot_rows(jnp.concatenate([high, low], axis=1), jnp.concatenate([other, other], axis=1))
         moments = jnp.transpose(moments)
         moments = moments[0:8] + moments[8:16] + moments[16:24]
         shift = jnp.where(
@@ -477,7 +481,7 @@
         charge = ext[1 + x, 1 + y, pl.ds(3, 1), pl.ds(128 * z, 128)]
         for k in range(3):
             far = fine_forces[cell][k] + spread[:, 128 * k : 128 * (k + 1)]
-            out_ref[k, x, y, pl.ds(z, 1), :] = force_ref[cell, pl.ds(k, 1), :] - 4.0 * charge * far
+            out_ref[k, x, z, pl.ds(y, 1), :] = force_ref[cell, pl.ds(k, 1), :] - 4.0 * charge * far
 
     for copy in lap_copies + halo_copies + fine_copies + relays + plane_copies:
         copy.wait_send()
@@ -492,7 +496,9 @@
         any_spec = pl.BlockSpec(memory_space=pl.ANY)
         vmem_spec = pl.BlockSpec(memory_space=pltpu.VMEM)
         planes = 4 * subs
-        return pl.pallas_call(
+        positions = jnp.transpose(positions, (0, 1, 3, 2, 4))
+        charges = jnp.transpose(charges, (0, 2, 1, 3))
+        forces = pl.pallas_call(
             functools.partial(kernel, spaces, subs),
             out_shape=jax.ShapeDtypeStruct(positions.shape, F32),
             in_specs=[vmem_spec, vmem_spec, pl.BlockSpec(memory_space=pltpu.SMEM), any_spec, any_spec, any_spec, vmem_spec, any_spec, any_spec, any_spec],
@@ -538,6 +544,7 @@
             jnp.asarray(place), jnp.asarray(spread[0]), jnp.asarray(spread[1]), jnp.asarray(ring), jnp.asarray(select),
             jnp.asarray(coarse[0]), jnp.asarray(coarse[1]),
         )
+        return jnp.transpose(forces, (0, 1, 3, 2, 4))
 
     in_specs = (
         P(None, "space", "sub", None, None),

time: 85.8 us -> 46 us (0.54)
  Pallas kernels: 81.5 us -> 44.5 us
  local copies, waits for them, and re-layouts: 3.97 us -> 1.33 us
    pallas_call x1, Pallas kernels: 81.5 us -> 44.5 us  [body(): pl.pallas_call(functools.partial(kernel, spaces, subs), out_shape=jax.Sha...]
    pallas_call x1 -> x0, local copies, waits for them, and re-layouts: 1.35 us -> none  [body(): pl.pallas_call(functools.partial(kernel, spaces, subs), out_shape=jax.Sha...]
    unnamed x2 -> x1, local copies, waits for them, and re-layouts: 2.61 us -> 1.33 us
where the time goes in v2:
time: 46 us; the launch traced here: 45.8 us
  Pallas kernels  44.5 us (97%)
  local copies, waits for them, and re-layouts  1.33 us (3%)
    pallas_call x1, Pallas kernels, body(): pl.pallas_call(functools.partial(kernel, spaces, subs), out_shape=jax.Sha...  44.5 us
    unnamed x1, local copies, waits for them, and re-layouts  1.33 us

profile of v2, /device:TPU:1, one launch (start us, length us, event | category | flops | bytes accessed | tf_op | source)
XLA Modules:
  0.0 45.8 jit_solution(13144225706615843534)
XLA Ops:
  0.0 44.5 %shard_map.100 = f32[3,2,3,2,128]{4,3,2,1,0:T(2,128)} custom-call(f32[3,2,3,2,128]{4,3,2,1,0:T(2,128)} %bitcast.4, f32[2,3,2,128]{3,2,1,0:T(2,128)} %bitcast.5, s32[2,2,3]{2,1,0:T(2,128)} %count_ref.1, bf16[512,128]{1,0:T(8,128)(2,1)} %constant.14.clone.place_hbm, bf16[256,1152]{1,0:T(8,128)(2,1)} %constant.15.clone.wide_hi_hbm, ...), custom_call_target="tpu_custom_call" | custom-call | tf_op jit(solution)/shard_map/pallas_call | solution.py:501
  44.5 1.3 %copy.12 = f32[3,2,2,3,128]{4,2,3,1,0:T(2,128)} copy(f32[3,2,2,3,128]{4,2,3,1,0:T(2,128)} %bitcast.3) | data formatting | bytes 36864

commit v3 on v2

--- a/solution.py
+++ b/solution.py
@@ -133,12 +133,12 @@
 
 def kernel(
     spaces, subs,
-    pos_ref, charge_ref, count_ref, place_hbm, wide_hi_hbm, wide_lo_hbm, ring_ref, select_hbm, far_hi_hbm, far_lo_hbm,
+    pos_hbm, charge_hbm, count_hbm, place_hbm, wide_hi_hbm, wide_lo_hbm, ring_hbm, select_hbm, far_hi_hbm, far_lo_hbm,
     out_ref,
-    place_ref, wide_hi, wide_lo, select_ref, far_hi, far_lo,
+    pos_ref, charge_ref, count_ref, ring_ref, place_ref, wide_hi, wide_lo, select_ref, far_hi, far_lo,
     ext, lap_buf, plane_out, plane_buf, fine_out, fine_buf,
-    fine_sum, by_ref, wz_ref, pair_hi, pair_lo, vx_ref, left_ref, right_ref, mom_ref, force_ref,
-    const_sem, halo_send, halo_recv, lap_send, lap_recv, relay_send, relay_recv, fine_send, fine_recv, plane_send, plane_recv,
+    fine_sum, by_ref, wz_ref, pair_hi, pair_lo, vx_ref, left_ref, right_ref, mom_ref, square_ref, raw_ref, back_ref, force_ref,
+    input_sem, const_sem, halo_send, halo_recv, lap_send, lap_recv, relay_send, relay_recv, fine_send, fine_recv, plane_send, plane_recv,
 ):
     laps = spaces // 4
     space = lax.axis_index("space")
@@ -151,10 +151,14 @@
         pltpu.make_async_copy(src, dst, const_sem.at[num])
         for num, (src, dst) in enumerate((
             (place_hbm, place_ref), (wide_hi_hbm, wide_hi), (wide_lo_hbm, wide_lo),
-            (select_hbm, select_ref), (far_hi_hbm, far_hi), (far_lo_hbm, far_lo),
+            (select_hbm, select_ref), (far_hi_hbm, far_hi), (far_lo_hbm, far_lo), (ring_hbm, ring_ref),
         ))
     ]
-    for load in loads:
+    inputs = [
+        pltpu.make_async_copy(src, dst, input_sem.at[num])
+        for num, (src, dst) in enumerate(((pos_hbm, pos_ref), (charge_hbm, charge_ref), (count_hbm, count_ref)))
+    ]
+    for load in inputs:
         load.start()
 
     def near_id(side):
@@ -178,6 +182,10 @@
     for member, step in members:
         pl.semaphore_signal(barrier, inc=1, device_id=plane_id(member, step), device_id_type=MESH)
 
+    for load in loads:
+        load.start()
+    for load in inputs:
+        load.wait()
     lane = lax.broadcasted_iota(jnp.int32, (1, 128), 1)
     for x in range(2):
         for y in range(2):
@@ -235,34 +243,6 @@
     total = total[0:8] + total[8:16]
     lap_buf[0] = total[:, 0:128] + total[:, 128:256]
 
-    pl.semaphore_wait(barrier, len(NEAR) + len(LAPS) + len(members))
-
-    lap_copies = []
-    for num, step in enumerate(LAPS):
-        copy = pltpu.make_async_remote_copy(
-            src_ref=lap_buf.at[0], dst_ref=lap_buf.at[(-step) % laps], send_sem=lap_send.at[num], recv_sem=lap_recv.at[num],
-            device_id=lap_id(step), device_id_type=MESH,
-        )
-        copy.start()
-        lap_copies.append(copy)
-
-    def piece(step, far):
-        if step == 0:
-            return pl.ds(1, 2)
-        if far:
-            return pl.ds(0 if step > 0 else 3, 1)
-        return pl.ds(2 if step > 0 else 1, 1)
-
-    halo_copies = []
-    for num, side in enumerate(NEAR):
-        copy = pltpu.make_async_remote_copy(
-            src_ref=ext.at[piece(side[0], False), piece(side[1], False)],
-            dst_ref=ext.at[piece(side[0], True), piece(side[1], True)],
-            send_sem=halo_send.at[num], recv_sem=halo_recv.at[num], device_id=near_id(side), device_id_type=MESH,
-        )
-        copy.start()
-        halo_copies.append(copy)
-
     fine_sum[...] = jnp.zeros_like(fine_sum)
 
     def fine_step(cell, carry):
@@ -298,6 +278,88 @@
     fine_all = fine_all[0:16] + fine_all[16:32] + dot(parts[0:16], wide_lo[...])
     for num in range(9):
         fine_out[num] = fine_all[:, 128 * num : 128 * (num + 1)]
+    row_w = row_iota(8, 640)
+    slot_w = lax.broadcasted_iota(jnp.int32, (8, 640), 1) // 128
+
+    def column_step(column, carry):
+        x, y = column // 4, column % 4
+        block = ext[x, y]
+        block = jnp.concatenate([block[:, 256:384], block, block[:, 0:128]], axis=1)
+        shift = jnp.where(
+            row_w == 0, (x - 2).astype(F32), jnp.where(row_w == 1, (y - 2).astype(F32), slot_w.astype(F32) - 2.5)
+        )
+        coords = jnp.where(row_w < 3, SPLIT_RATE * (block + shift), 0.0)
+        square = jnp.sum(coords * coords, axis=0, keepdims=True) + SPLIT_RATE * SPLIT_RATE * SOFT_SQUARE
+        ones = jnp.where(row_w == 3, 1.0, 0.0)
+        p1, p2, p3 = thirds(coords)
+        s1, s2, s3 = thirds(square)
+
+        def with_square(part, square_part):
+            return jnp.where(row_w == 4, square_part, part + ones)
+
+        right_ref[column] = jnp.concatenate(
+            [with_square(p1, s1), with_square(p2, s2), with_square(p1, s3), p3, p2, p1], axis=0
+        ).astype(BF16)
+        moments = (coords + ones) * block[3:4]
+        m1, m2, m3 = thirds(moments)
+        mom_ref[column] = jnp.concatenate([m1, m2, m3, jnp.zeros_like(m1)], axis=0).astype(BF16)
+        return carry
+
+    for column in (5, 6, 9, 10):
+        column_step(jnp.int32(column), 0)
+
+    row_c = row_iota(8)
+
+    def left_step(cell, carry):
+        x, y, z, block = cell_rows(cell)
+        shift = jnp.where(
+            row_c == 0, (x - 1).astype(F32), jnp.where(row_c == 1, (y - 1).astype(F32), z.astype(F32) - 1.5)
+        )
+        coords = jnp.where(row_c < 3, SPLIT_RATE * (block + shift), 0.0)
+        square = jnp.sum(coords * coords, axis=0, keepdims=True)
+        ones = jnp.where(row_c == 4, 1.0, 0.0)
+        p1, p2, p3 = thirds(-2.0 * coords)
+        s1, s2, s3 = thirds(square)
+
+        def with_square(part, square_part):
+            return jnp.where(row_c == 3, square_part, part + ones)
+
+        stacked = jnp.concatenate(
+            [with_square(p1, s1), with_square(p1, s2), with_square(p2, s3), p1, p2, p3, jnp.zeros((80, 128), F32)], axis=0
+        )
+        left_ref[cell] = jnp.transpose(stacked).astype(BF16)
+        return carry
+
+    grouped(6, left_step, 0)
+
+    pl.semaphore_wait(barrier, len(NEAR) + len(LAPS) + len(members))
+
+    lap_copies = []
+    for num, step in enumerate(LAPS):
+        copy = pltpu.make_async_remote_copy(
+            src_ref=lap_buf.at[0], dst_ref=lap_buf.at[(-step) % laps], send_sem=lap_send.at[num], recv_sem=lap_recv.at[num],
+            device_id=lap_id(step), device_id_type=MESH,
+        )
+        copy.start()
+        lap_copies.append(copy)
+
+    def piece(step, far):
+        if step == 0:
+            return pl.ds(1, 2)
+        if far:
+            return pl.ds(0 if step > 0 else 3, 1)
+        return pl.ds(2 if step > 0 else 1, 1)
+
+    halo_copies = []
+    for num, side in enumerate(NEAR):
+        copy = pltpu.make_async_remote_copy(
+            src_ref=ext.at[piece(side[0], False), piece(side[1], False)],
+            dst_ref=ext.at[piece(side[0], True), piece(side[1], True)],
+            send_sem=halo_send.at[num], recv_sem=halo_recv.at[num], device_id=near_id(side), device_id_type=MESH,
+        )
+        copy.start()
+        halo_copies.append(copy)
+
     fine_copies = []
     for num, side in enumerate(NEAR):
         copy = pltpu.make_async_remote_copy(
@@ -306,6 +368,105 @@
         )
         copy.start()
         fine_copies.append(copy)
+
+
+    def outer_columns(cell):
+        x, y = cell // 6, (cell // 3) % 2
+        return [12 * x + y + num for num in range(3)] + [3 * y + 4, 3 * y + 8]
+
+    def slot_lanes(slot, count=1):
+        return pl.ds(pl.multiple_of(slot * 128, 128), 128 * count)
+
+    def pull(square):
+        inverse = lax.rsqrt(square)
+        far = 1.0 - lax.erf(square * inverse)
+        bell = jnp.exp2(square * (-math.log2(math.e)))
+        factor = (inverse * inverse) * (far * inverse + (2.0 / math.sqrt(math.pi)) * bell)
+        high = factor.astype(BF16)
+        return high, (factor - high.astype(F32)).astype(BF16)
+
+    def gather_moments(moments, high, low, other):
+        return moments + dot_rows(jnp.concatenate([high, low], axis=1), jnp.concatenate([other, other], axis=1))
+
+    inner_ids = (5, 6, 9, 10)
+
+    def inner_squares(z, half):
+        at = 0
+        for one in range(4):
+            left = left_ref[3 * one + z][:, 0:48]
+            own = inner_ids[one]
+            square_ref[half, :, 128 * at : 128 * (at + 2)] = dot(left, right_ref[own, :, slot_lanes(z + 1, 2)])
+            at += 2
+            for other in range(one + 1, 4):
+                column = inner_ids[other]
+                square_ref[half, :, 128 * at : 128 * (at + 3)] = dot(left, right_ref[column, :, slot_lanes(z, 3)])
+                at += 3
+
+    def inner_pulls(z, half):
+        at = 0
+        for one in range(4):
+            own = inner_ids[one]
+            moments = jnp.zeros((128, 32), F32)
+            units = [(one, 1), (one, 2)] + [(other, slot) for other in range(one + 1, 4) for slot in range(3)]
+            for other, slot in units:
+                high, low = pull(square_ref[half, :, 128 * at : 128 * (at + 1)])
+                at += 1
+                moments = gather_moments(moments, high, low, mom_ref[inner_ids[other], :, slot_lanes(z + slot)])
+                if (other, slot) != (one, 1):
+                    z_other = (z + slot + 2) % 3
+                    back = mom_ref[own, :, slot_lanes(z_other + 2 - slot)]
+                    cell = 3 * other + z_other
+                    back_ref[cell] += dot(jnp.concatenate([back, back], axis=1), jnp.concatenate([high, low], axis=0))
+            raw_ref[3 * one + z] = moments
+
+    def inner_sweep(start, stop):
+        inner_squares(jnp.int32(start), 0)
+        for z in range(start, stop):
+            if z + 1 < stop:
+                inner_squares(jnp.int32(z + 1), (z + 1 - start) % 2)
+            inner_pulls(jnp.int32(z), (z - start) % 2)
+
+    def outer_squares(cell, half):
+        left = left_ref[cell][:, 0:48]
+        lanes = slot_lanes(cell % 3, 3)
+        for num, column in enumerate(outer_columns(cell)):
+            square_ref[half, :, 384 * num : 384 * (num + 1)] = dot(left, right_ref[column, :, lanes])
+
+    def outer_pulls(cell, half):
+        moments = raw_ref[cell]
+        for num, column in enumerate(outer_columns(cell)):
+            for slot in range(3):
+                at = 384 * num + 128 * slot
+                high, low = pull(square_ref[half, :, at : at + 128])
+                moments = gather_moments(moments, high, low, mom_ref[column, :, slot_lanes(cell % 3 + slot)])
+        raw_ref[cell] = moments
+
+    def outer_sweep(start, stop):
+        outer_squares(start, 0)
+
+        def step(num, carry):
+            for part in range(4):
+                cell = start + 4 * num + part
+                outer_squares(jnp.minimum(cell + 1, stop - 1), (part + 1) % 2)
+                outer_pulls(cell, part % 2)
+            return carry
+
+        lax.fori_loop(0, (stop - start) // 4, step, 0)
+
+    def finish_step(cell, carry):
+        x, y, z, block = cell_rows(cell)
+        moments = jnp.transpose(raw_ref[cell])
+        moments = moments + back_ref[cell]
+        moments = moments[0:8] + moments[8:16] + moments[16:24]
+        shift = jnp.where(
+            row_c == 0, (x - 1).astype(F32), jnp.where(row_c == 1, (y - 1).astype(F32), z.astype(F32) - 1.5)
+        )
+        coords = SPLIT_RATE * (block + shift)
+        force_ref[cell] = (SPLIT_RATE * SPLIT_RATE) * block[3:4] * (coords * moments[3:4] - moments)
+        return carry
+
+    back_ref[...] = jnp.zeros_like(back_ref)
+    inner_sweep(0, 3)
 
     for copy in lap_copies:
         copy.wait_recv()
@@ -321,89 +482,15 @@
         copy.start()
         relays.append(copy)
 
+
     for copy in halo_copies:
         copy.wait_recv()
 
-    row_w = row_iota(8, 640)
-    slot_w = lax.broadcasted_iota(jnp.int32, (8, 640), 1) // 128
-
-    def column_step(column, carry):
-        x, y = column // 4, column % 4
-        block = ext[x, y]
-        block = jnp.concatenate([block[:, 256:384], block, block[:, 0:128]], axis=1)
-        shift = jnp.where(
-            row_w == 0, (x - 2).astype(F32), jnp.where(row_w == 1, (y - 2).astype(F32), slot_w.astype(F32) - 2.5)
-        )
-        coords = jnp.where(row_w < 3, SPLIT_RATE * (block + shift), 0.0)
-        square = jnp.sum(coords * coords, axis=0, keepdims=True) + SPLIT_RATE * SPLIT_RATE * SOFT_SQUARE
-        ones = jnp.where(row_w == 3, 1.0, 0.0)
-        p1, p2, p3 = thirds(coords)
-        s1, s2, s3 = thirds(square)
-
-        def with_square(part, square_part):
-            return jnp.where(row_w == 4, square_part, part + ones)
-
-        right_ref[column] = jnp.concatenate(
-            [with_square(p1, s1), with_square(p2, s2), with_square(p1, s3), p3, p2, p1], axis=0
-        ).astype(BF16)
-        moments = (coords + ones) * block[3:4]
-        m1, m2, m3 = thirds(moments)
-        mom_ref[column] = jnp.concatenate([m1, m2, m3, jnp.zeros_like(m1)], axis=0).astype(BF16)
-        return carry
-
-    lax.fori_loop(0, 16, column_step, 0)
-
-    row_c = row_iota(8)
-
-    def left_step(cell, carry):
-        x, y, z, block = cell_rows(cell)
-        shift = jnp.where(
-            row_c == 0, (x - 1).astype(F32), jnp.where(row_c == 1, (y - 1).astype(F32), z.astype(F32) - 1.5)
-        )
-        coords = jnp.where(row_c < 3, SPLIT_RATE * (block + shift), 0.0)
-        square = jnp.sum(coords * coords, axis=0, keepdims=True)
-        ones = jnp.where(row_c == 4, 1.0, 0.0)
-        p1, p2, p3 = thirds(-2.0 * coords)
-        s1, s2, s3 = thirds(square)
-
-        def with_square(part, square_part):
-            return jnp.where(row_c == 3, square_part, part + ones)
-
-        stacked = jnp.concatenate(
-            [with_square(p1, s1), with_square(p1, s2), with_square(p2, s3), p1, p2, p3, jnp.zeros((80, 128), F32)], axis=0
-        )
-        left_ref[cell] = jnp.transpose(stacked).astype(BF16)
-        return carry
-
-    grouped(6, left_step, 0)
-
-    def pair_step(cell, carry):
-        x, y, z, block = cell_rows(cell)
-        left = left_ref[cell][:, 0:48]
-
-        moments = jnp.zeros((128, 32), F32)
-        lanes = pl.ds(pl.multiple_of(z * 128, 128), 384)
-        for side in range(9):
-            column = (x + side // 3) * 4 + y + side % 3
-            square = dot(left, right_ref[column, :, lanes])
-            inverse = lax.rsqrt(square)
-            far = 1.0 - lax.erf(square * inverse)
-            bell = jnp.exp2(square * (-math.log2(math.e)))
-            factor = (inverse * inverse) * (far * inverse + (2.0 / math.sqrt(math.pi)) * bell)
-            high = factor.astype(BF16)
-            low = (factor - high.astype(F32)).astype(BF16)
-            other = mom_ref[column, :, lanes]
-            moments = moments + dot_rows(jnp.concatenate([high, low], axis=1), jnp.concatenate([other, other], axis=1))
-        moments = jnp.transpose(moments)
-        moments = moments[0:8] + moments[8:16] + moments[16:24]
-        shift = jnp.where(
-            row_c == 0, (x - 1).astype(F32), jnp.where(row_c == 1, (y - 1).astype(F32), z.astype(F32) - 1.5)
-        )
-        coords = SPLIT_RATE * (block + shift)
-        force_ref[cell] = (SPLIT_RATE * SPLIT_RATE) * block[3:4] * (coords * moments[3:4] - moments)
-        return carry
-
-    lax.fori_loop(0, 4, pair_step, 0)
+    def rim_step(num, carry):
+        return column_step(num + jnp.where(num > 4, 2, 0) + jnp.where(num > 6, 2, 0), carry)
+
+    lax.fori_loop(0, 12, rim_step, 0)
+    outer_sweep(0, 4)
 
     for copy in relays:
         copy.wait_recv()
@@ -438,7 +525,8 @@
         copy.start()
         plane_copies.append(copy)
 
-    lax.fori_loop(4, CELLS, pair_step, 0)
+    outer_sweep(4, CELLS)
+    grouped(6, finish_step, 0)
 
     for copy in fine_copies:
         copy.wait_recv()
@@ -501,9 +589,13 @@
         forces = pl.pallas_call(
             functools.partial(kernel, spaces, subs),
             out_shape=jax.ShapeDtypeStruct(positions.shape, F32),
-            in_specs=[vmem_spec, vmem_spec, pl.BlockSpec(memory_space=pltpu.SMEM), any_spec, any_spec, any_spec, vmem_spec, any_spec, any_spec, any_spec],
+            in_specs=[any_spec] * 10,
             out_specs=vmem_spec,
             scratch_shapes=[
+                pltpu.VMEM((3, 2, 3, 2, 128), F32),
+                pltpu.VMEM((2, 3, 2, 128), F32),
+                pltpu.SMEM((2, 2, 3), jnp.int32),
+                pltpu.VMEM((32, 16), F32),
                 pltpu.VMEM((512, 128), BF16),
                 pltpu.VMEM((256, 1152), BF16),
                 pltpu.VMEM((256, 1152), BF16),
@@ -525,8 +617,12 @@
                 pltpu.VMEM((CELLS, 128, 128), BF16),
                 pltpu.VMEM((16, 48, 640), BF16),
                 pltpu.VMEM((16, 32, 640), BF16),
+                pltpu.VMEM((2, 128, 3328), F32),
+                pltpu.VMEM((CELLS, 128, 32), F32),
+                pltpu.VMEM((CELLS, 32, 128), F32),
                 pltpu.VMEM((CELLS, 8, 128), F32),
-                pltpu.SemaphoreType.DMA((6,)),
+                pltpu.SemaphoreType.DMA((3,)),
+                pltpu.SemaphoreType.DMA((7,)),
                 pltpu.SemaphoreType.DMA((8,)),
                 pltpu.SemaphoreType.DMA((8,)),
                 pltpu.SemaphoreType.DMA((8,)),

time: 46 us -> 35 us (0.76)
  Pallas kernels: 44.5 us -> 33.4 us
    pallas_call x1, Pallas kernels: 44.5 us -> 33.4 us  [body(): pl.pallas_call(functools.partial(kernel, spaces, subs), out_shape=jax.Sha...]
where the time goes in v3:
time: 35 us; the launch traced here: 34.8 us
  Pallas kernels  33.4 us (95%)
  local copies, waits for them, and re-layouts  1.33 us (4%)
    pallas_call x1, Pallas kernels, body(): pl.pallas_call(functools.partial(kernel, spaces, subs), out_shape=jax.Sha...  33.4 us
    unnamed x1, local copies, waits for them, and re-layouts  1.33 us

profile of v3, /device:TPU:1, one launch (start us, length us, event | category | flops | bytes accessed | tf_op | source)
XLA Modules:
  0.0 34.8 jit_solution(7057621782981328389)
XLA Ops:
  0.0 33.4 %shard_map.100 = f32[3,2,3,2,128]{4,3,2,1,0:T(2,128)} custom-call(f32[3,2,3,2,128]{4,3,2,1,0:T(2,128)} %bitcast.4, f32[2,3,2,128]{3,2,1,0:T(2,128)} %bitcast.5, s32[2,2,3]{2,1,0:T(2,128)} %count_hbm.1, bf16[512,128]{1,0:T(8,128)(2,1)} %constant.14.clone.place_hbm, bf16[256,1152]{1,0:T(8,128)(2,1)} %constant.15.clone.wide_hi_hbm, ...), custom_call_target="tpu_custom_call" | custom-call | tf_op jit(solution)/shard_map/pallas_call | solution.py:589
  33.4 1.3 %copy.12 = f32[3,2,2,3,128]{4,2,3,1,0:T(2,128)} copy(f32[3,2,2,3,128]{4,2,3,1,0:T(2,128)} %bitcast.3) | data formatting | bytes 36864

commit v4 on v2

--- a/solution.py
+++ b/solution.py
@@ -24,6 +24,24 @@
 NEAR = [side for side in SIDES if side != (0, 0)]
 LAPS = (1, 2, 3, 4, -1, -2, -3, -4)
 CELLS = 12
+INNER = (5, 6, 9, 10)
+AHEAD = ((1, 0), (0, 1), (1, 1), (1, -1), (0, -1))
+FROM = (((1, 1), (1, 2)), ((1, 1), (2, 1)), ((1, 1),), ((1, 2),), ((2, 2),))
+INTO = (((3, 1), (3, 2)), ((1, 3), (2, 3)), ((3, 3),), ((3, 0),), ((2, 0),))
+RIM = tuple(4 * x + y for group in INTO for x, y in group)
+INNER_PLAN = [
+    [(INNER[one], (1, 2))] + [(INNER[other], (0, 1, 2)) for other in range(one + 1, 4)] for one in range(4)
+]
+OUTER_PLAN = [
+    [
+        (4 * (1 + x + dx) + 1 + y + dy, (0, 1, 2))
+        for dx, dy in ((1, -1), (1, 0), (1, 1), (0, 1))
+        if x + dx > 1 or not 0 <= y + dy <= 1
+    ]
+    for x in range(2)
+    for y in range(2)
+]
+LOG2E = math.log2(math.e)
 
 
 def two_parts(table):
@@ -65,7 +83,7 @@
                 select[y, x, f, 11 * x + 4 * y + f] = 1.0
     select = select.reshape(192, 128).astype(jnp.bfloat16)
     total_y = 4 * sub_size
-    coarse = np.zeros((2, 8, 8, sub_size, 16, 8), np.float32)
+    coarse = np.zeros((2, 2, 8, 8, sub_size, 2, 8, 8), np.float32)
     for number, (fraction, weight) in enumerate(zip(COARSE_FRACTIONS, COARSE_WEIGHTS)):
         dist = np.abs(np.arange(6)[:, None] - np.arange(6)[None, :])
         dist = np.minimum(dist, 6 - dist).astype(np.float64)
@@ -75,8 +93,9 @@
             dist = np.minimum(dist, total_y - dist).astype(np.float64)
             along_y = np.exp(-dist * dist / (2 * (total_y / fraction) ** 2))
             both = 0.125 * weight * along_z[:, None, :, None] * along_y[None, :, None, :]
-            coarse[number, :6, :6, step, :6, :6] = both
-    coarse = two_parts(coarse.reshape(128, sub_size * 128))
+            for half in range(2):
+                coarse[half, number, :6, :6, step, half, :6, :6] = both
+    coarse = two_parts(coarse.reshape(256, sub_size * 128))
     return place, spread, ring, select, coarse
 
 
@@ -133,12 +152,12 @@
 
 def kernel(
     spaces, subs,
-    pos_ref, charge_ref, count_ref, place_hbm, wide_hi_hbm, wide_lo_hbm, ring_ref, select_hbm, far_hi_hbm, far_lo_hbm,
+    pos_hbm, charge_hbm, count_hbm, place_hbm, wide_hi_hbm, wide_lo_hbm, ring_hbm, select_hbm, far_hi_hbm, far_lo_hbm,
     out_ref,
-    place_ref, wide_hi, wide_lo, select_ref, far_hi, far_lo,
+    pos_ref, charge_ref, count_ref, ring_ref, place_ref, wide_hi, wide_lo, select_ref, far_hi, far_lo,
     ext, lap_buf, plane_out, plane_buf, fine_out, fine_buf,
-    fine_sum, by_ref, wz_ref, pair_hi, pair_lo, vx_ref, left_ref, right_ref, mom_ref, force_ref,
-    const_sem, halo_send, halo_recv, lap_send, lap_recv, relay_send, relay_recv, fine_send, fine_recv, plane_send, plane_recv,
+    fine_sum, by_ref, wz_ref, pair_hi, pair_lo, vx_ref, bells_ref, left_ref, right_ref, mom_ref, square_ref, bell_ref, raw_ref, back_ref, return_out, return_buf, force_ref,
+    input_sem, const_sem, halo_send, halo_recv, lap_send, lap_recv, relay_send, relay_recv, return_send, return_recv, fine_send, fine_recv, plane_send, plane_recv,
 ):
     laps = spaces // 4
     space = lax.axis_index("space")
@@ -151,10 +170,14 @@
         pltpu.make_async_copy(src, dst, const_sem.at[num])
         for num, (src, dst) in enumerate((
             (place_hbm, place_ref), (wide_hi_hbm, wide_hi), (wide_lo_hbm, wide_lo),
-            (select_hbm, select_ref), (far_hi_hbm, far_hi), (far_lo_hbm, far_lo),
+            (select_hbm, select_ref), (far_hi_hbm, far_hi), (far_lo_hbm, far_lo), (ring_hbm, ring_ref),
         ))
     ]
-    for load in loads:
+    inputs = [
+        pltpu.make_async_copy(src, dst, input_sem.at[num])
+        for num, (src, dst) in enumerate(((pos_hbm, pos_ref), (charge_hbm, charge_ref), (count_hbm, count_ref)))
+    ]
+    for load in inputs:
         load.start()
 
     def near_id(side):
@@ -178,6 +201,10 @@
     for member, step in members:
         pl.semaphore_signal(barrier, inc=1, device_id=plane_id(member, step), device_id_type=MESH)
 
+    for load in loads:
+        load.start()
+    for load in inputs:
+        load.wait()
     lane = lax.broadcasted_iota(jnp.int32, (1, 128), 1)
     for x in range(2):
         for y in range(2):
@@ -187,36 +214,49 @@
                     ext[1 + x, 1 + y, pl.ds(k, 1), lanes] = pos_ref[k, x, z, pl.ds(y, 1), :]
                 live = lane < count_ref[x, y, z]
                 ext[1 + x, 1 + y, pl.ds(3, 1), lanes] = jnp.where(live, charge_ref[x, z, pl.ds(y, 1), :], 0.0)
-            ext[1 + x, 1 + y, pl.ds(4, 4), :] = jnp.zeros((4, 384), F32)
 
     def cell_rows(cell):
         x, y, z = cell // 6, (cell // 3) % 2, cell % 3
-        block = ext[1 + x, 1 + y, :, pl.ds(pl.multiple_of(z * 128, 128), 128)]
-        return x, y, z, block
+        at = 128 * z if isinstance(z, int) else pl.multiple_of(z * 128, 128)
+        return x, y, z, ext[1 + x, 1 + y, :, pl.ds(at, 128)]
+
+    def real(value):
+        return float(value) if isinstance(value, int) else value.astype(F32)
+
+    def padded(block):
+        return jnp.concatenate([block, jnp.zeros_like(block)], axis=0)
 
     row8 = row_iota(8).astype(F32)
     row16 = row_iota(16).astype(F32)
 
-    def coarse_step(cell, total):
+    row_map = jnp.where(row8 > 3.0, row8 - 1.0, row8)
+    row_live = (row8 != 3.0) & (row8 != 7.0)
+
+    def coarse_weights(cell, shape):
         x, y, z, block = cell_rows(cell)
-        at_x = 4.0 * block[0:1] + (4 * x + 2).astype(F32) - 2.0 * row8
-        at_y = 4.0 * block[1:2] + (4 * y + 2).astype(F32) - 2.0 * row8
-        at_z = 4.0 * block[2:3] + (4 * z).astype(F32) - 2.0 * row8
-        charge = block[3:4]
-        near_z, next_z = wrapped(at_z), wrapped(at_z - 1.0)
-        some = row8 < 6.0
-        vx = spline(at_x) + spline(at_x - 1.0)
-        vy = spline(at_y) + spline(at_y - 1.0)
-        vz = jnp.where(some, spline(near_z) + spline(next_z), 0.0)
-        sx = spline_slope(at_x) + spline_slope(at_x - 1.0)
-        sy = spline_slope(at_y) + spline_slope(at_y - 1.0)
-        sz = jnp.where(some, spline_slope(near_z) + spline_slope(next_z), 0.0)
-        vz_charge = vz * charge
-        pad = jnp.zeros((16, 128), F32)
-        product = jnp.concatenate([vz_charge[k : k + 1] * vy for k in range(6)], axis=0)
-        high, low = halves(product)
+        at_x = 4.0 * block[0:1] + real(4 * x + 2) - 2.0 * row_map
+        at_y = 4.0 * block[1:2] + real(4 * y + 2) - 2.0 * row8
+        at_z = 4.0 * block[2:3] + real(4 * z) - 2.0 * row8
+        vx = jnp.where(row_live, shape(at_x) + shape(at_x - 1.0), 0.0)
+        vy = shape(at_y) + shape(at_y - 1.0)
+        vz = jnp.where(row8 < 6.0, shape(wrapped(at_z)) + shape(wrapped(at_z - 1.0)), 0.0)
+        return vx, vy, vz, block[3:4]
+
+    pad = jnp.zeros((16, 128), F32)
+    total = jnp.zeros((16, 256), F32)
+    for cell in range(CELLS):
+        vx, vy, vz, charge = coarse_weights(cell, spline)
+        vz = vz * charge
+        high, low = halves(jnp.concatenate([vz[k : k + 1] * vy for k in range(6)], axis=0))
         right = jnp.concatenate([high, pad, high, pad, low, pad, low, pad], axis=0).astype(BF16)
-        left = jnp.concatenate(halves(vx), axis=0).astype(BF16)
+        total = total + dot_rows(jnp.concatenate(halves(vx), axis=0).astype(BF16), right)
+    total = total[0:8] + total[8:16]
+    total = total[:, 0:128] + total[:, 128:256]
+    lap_buf[0] = jnp.where(lane < 64, total[0:4], total[4:8])
+
+    def tables_step(cell, carry):
+        vx, vy, vz, charge = coarse_weights(cell, spline)
+        sx, sy, sz, charge = coarse_weights(cell, spline_slope)
         lanes = pl.ds(pl.multiple_of(cell * 384, 128), 384)
         tables = jnp.concatenate(
             [
@@ -229,11 +269,7 @@
         pair_hi[:, lanes] = high.astype(BF16)
         pair_lo[:, lanes] = low.astype(BF16)
         vx_ref[:, lanes] = jnp.concatenate([sx, vx, vx], axis=1)
-        return total + dot_rows(left, right)
-
-    total = grouped(6, coarse_step, jnp.zeros((16, 256), F32))
-    total = total[0:8] + total[8:16]
-    lap_buf[0] = total[:, 0:128] + total[:, 128:256]
+        return carry
 
     pl.semaphore_wait(barrier, len(NEAR) + len(LAPS) + len(members))
 
@@ -246,22 +282,136 @@
         copy.start()
         lap_copies.append(copy)
 
-    def piece(step, far):
-        if step == 0:
-            return pl.ds(1, 2)
-        if far:
-            return pl.ds(0 if step > 0 else 3, 1)
-        return pl.ds(2 if step > 0 else 1, 1)
-
     halo_copies = []
-    for num, side in enumerate(NEAR):
+    for num, side in enumerate(AHEAD):
+        (x, y), (to_x, to_y) = FROM[num][0], INTO[num][0]
+        span_x, span_y = FROM[num][-1][0] - x + 1, FROM[num][-1][1] - y + 1
         copy = pltpu.make_async_remote_copy(
-            src_ref=ext.at[piece(side[0], False), piece(side[1], False)],
-            dst_ref=ext.at[piece(side[0], True), piece(side[1], True)],
-            send_sem=halo_send.at[num], recv_sem=halo_recv.at[num], device_id=near_id(side), device_id_type=MESH,
+            src_ref=ext.at[pl.ds(x, span_x), pl.ds(y, span_y)], dst_ref=ext.at[pl.ds(to_x, span_x), pl.ds(to_y, span_y)],
+            send_sem=halo_send.at[num], recv_sem=halo_recv.at[num],
+            device_id=near_id((-side[0], -side[1])), device_id_type=MESH,
         )
         copy.start()
         halo_copies.append(copy)
+
+    row_w = row_iota(8, 640)
+    slot_w = lax.broadcasted_iota(jnp.int32, (8, 640), 1) // 128
+
+    def column_step(column, carry):
+        x, y = column // 4, column % 4
+        block = ext[x, y]
+        block = padded(jnp.concatenate([block[:, 256:384], block, block[:, 0:128]], axis=1))
+        shift = jnp.where(
+            row_w == 0, (x - 2).astype(F32), jnp.where(row_w == 1, (y - 2).astype(F32), slot_w.astype(F32) - 2.5)
+        )
+        coords = jnp.where(row_w < 3, SPLIT_RATE * (block + shift), 0.0)
+        square = jnp.sum(coords * coords, axis=0, keepdims=True) + SPLIT_RATE * SPLIT_RATE * SOFT_SQUARE
+        ones = jnp.where(row_w == 3, 1.0, 0.0)
+        p1, p2, p3 = thirds(coords)
+        squares_of = thirds(square)
+        bells_of = thirds(-LOG2E * square)
+
+        def with_square(part, num):
+            return jnp.where(row_w == 4, squares_of[num], jnp.where(row_w == 5, bells_of[num], part + ones))
+
+        right_ref[column] = jnp.concatenate(
+            [with_square(p1, 0), with_square(p2, 1), with_square(p1, 2), p3, p2, p1], axis=0
+        ).astype(BF16)
+        moments = (coords + ones) * block[3:4]
+        m1, m2, m3 = thirds(moments)
+        mom_ref[column] = jnp.concatenate([m1, m2, m3, jnp.zeros_like(m1)], axis=0).astype(BF16)
+        return carry
+
+    for column in (5, 6, 9, 10):
+        column_step(jnp.int32(column), 0)
+
+    row_c = row_iota(8)
+
+    def left_step(cell, carry):
+        x, y, z, block = cell_rows(cell)
+        block = padded(block)
+        shift = jnp.where(
+            row_c == 0, (x - 1).astype(F32), jnp.where(row_c == 1, (y - 1).astype(F32), z.astype(F32) - 1.5)
+        )
+        coords = jnp.where(row_c < 3, SPLIT_RATE * (block + shift), 0.0)
+        square = jnp.sum(coords * coords, axis=0, keepdims=True)
+
+        def features(cross, own, ones_row):
+            ones = jnp.where(row_c == ones_row, 1.0, 0.0)
+            p1, p2, p3 = thirds(cross)
+            q1, q2, q3 = [jnp.where(row_c == 3, part, ones) for part in thirds(own)]
+            return jnp.concatenate([p1 + q1, p1 + q2, p2 + q3, p1, p2, p3, jnp.zeros((80, 128), F32)], axis=0)
+
+        left_ref[cell, 0:128, :] = jnp.transpose(features(-2.0 * coords, square, 4)).astype(BF16)
+        bell_own = math.log2(2.0 / math.sqrt(math.pi)) - LOG2E * square
+        left_ref[cell, 128:256, :] = jnp.transpose(features((2.0 * LOG2E) * coords, bell_own, 5)).astype(BF16)
+        return carry
+
+    grouped(6, left_step, 0)
+
+    def slot_lanes(slot, count=1):
+        return pl.ds(pl.multiple_of(slot * 128, 128), 128 * count)
+
+    def squares(plan, z, half):
+        at = 0
+        for one in range(4):
+            left = left_ref[3 * one + z][:, 0:48]
+            for column, slots in plan[one]:
+                both = dot(left, right_ref[column, :, slot_lanes(z + slots[0], len(slots))])
+                lanes = slice(128 * at, 128 * (at + len(slots)))
+                square_ref[half, :, lanes] = both[0:128]
+                bell_ref[half, :, lanes] = both[128:256]
+                at += len(slots)
+
+    def pulls(plan, z, half, first):
+        at = 0
+        for one in range(4):
+            own = INNER[one]
+            moments = jnp.zeros((128, 32), F32) if first else raw_ref[3 * one + z]
+            for column, slot in [(column, slot) for column, slots in plan[one] for slot in slots]:
+                square = square_ref[half, :, 128 * at : 128 * (at + 1)]
+                inverse = lax.rsqrt(square)
+                far = 1.0 - lax.erf(square * inverse)
+                factor = (inverse * inverse) * (far * inverse + jnp.exp2(bell_ref[half, :, 128 * at : 128 * (at + 1)]))
+                high = factor.astype(BF16)
+                low = (factor - high.astype(F32)).astype(BF16)
+                other = mom_ref[column, :, slot_lanes(z + slot)]
+                moments = moments + dot_rows(jnp.concatenate([high, low], axis=1), jnp.concatenate([other, other], axis=1))
+                if (column, slot) != (own, 1):
+                    z_other = (z + slot + 2) % 3
+                    back = mom_ref[own, :, slot_lanes(z_other + 2 - slot)]
+                    back_ref[3 * column + z_other] += dot(
+                        jnp.concatenate([back, back], axis=1), jnp.concatenate([high, low], axis=0)
+                    )
+                at += 1
+            raw_ref[3 * one + z] = moments
+
+    def sweep(plan, start, stop, first):
+        squares(plan, start, 0)
+        for z in range(start, stop):
+            if z + 1 < stop:
+                squares(plan, z + 1, (z + 1 - start) % 2)
+            pulls(plan, z, (z - start) % 2, first)
+
+    def summed(rows):
+        return rows[0:8] + rows[8:16] + rows[16:24]
+
+    def finish(cell):
+        x, y, z = cell // 6, (cell // 3) % 2, cell % 3
+        block = padded(ext[1 + x, 1 + y, :, 128 * z : 128 * (z + 1)])
+        moments = summed(jnp.transpose(raw_ref[cell]) + back_ref[3 * INNER[2 * x + y] + z])
+        for num, group in enumerate(FROM):
+            for place, column in enumerate(group):
+                if column == (1 + x, 1 + y):
+                    moments = moments + padded(return_buf[num, place, :, 128 * z : 128 * (z + 1)])
+        shift = jnp.where(row_c == 0, x - 1.0, jnp.where(row_c == 1, y - 1.0, z - 1.5))
+        coords = SPLIT_RATE * (block + shift)
+        force_ref[cell] = (SPLIT_RATE * SPLIT_RATE) * block[3:4] * (coords * moments[3:4] - moments)
+
+    back_ref[...] = jnp.zeros_like(back_ref)
+    for one in range(4):
+        raw_ref[3 * one + 2] = jnp.zeros((128, 32), F32)
+    sweep(INNER_PLAN, 0, 2, True)
 
     fine_sum[...] = jnp.zeros_like(fine_sum)
 
@@ -307,6 +457,21 @@
         copy.start()
         fine_copies.append(copy)
 
+
+    rows = lax.broadcasted_iota(jnp.int32, (128, 64), 0)
+    cols = lax.broadcasted_iota(jnp.int32, (128, 64), 1)
+    member = (rows // 4) % 4
+    to_space = ((outer_x + member // 2) % 2) * 2 * laps + lap * 2 + (core + member % 2) % 2
+    from_space = outer_x * 2 * laps + ((lap + cols // 4) % laps) * 2 + core
+    total_x = 4 * spaces
+    to_row = 3 * ((rows // 16) % 2) + rows % 4
+    from_row = 3 * (rows // 64) + cols % 4
+    dist = (4 * (to_space - from_space) + to_row - from_row + 2 * total_x) % total_x
+    dist = jnp.minimum(dist, total_x - dist).astype(F32)
+    wide = [2.0 * (total_x / fraction) ** 2 for fraction in COARSE_FRACTIONS]
+    bells = jnp.exp(-dist * dist * jnp.where((rows // 32) % 2 == 0, 1.0 / wide[0], 1.0 / wide[1]))
+    bells_ref[...] = jnp.concatenate(halves(bells), axis=0).astype(BF16)
+
     for copy in lap_copies:
         copy.wait_recv()
     relays = []
@@ -323,111 +488,38 @@
 
     for copy in halo_copies:
         copy.wait_recv()
-
-    row_w = row_iota(8, 640)
-    slot_w = lax.broadcasted_iota(jnp.int32, (8, 640), 1) // 128
-
-    def column_step(column, carry):
-        x, y = column // 4, column % 4
-        block = ext[x, y]
-        block = jnp.concatenate([block[:, 256:384], block, block[:, 0:128]], axis=1)
-        shift = jnp.where(
-            row_w == 0, (x - 2).astype(F32), jnp.where(row_w == 1, (y - 2).astype(F32), slot_w.astype(F32) - 2.5)
-        )
-        coords = jnp.where(row_w < 3, SPLIT_RATE * (block + shift), 0.0)
-        square = jnp.sum(coords * coords, axis=0, keepdims=True) + SPLIT_RATE * SPLIT_RATE * SOFT_SQUARE
-        ones = jnp.where(row_w == 3, 1.0, 0.0)
-        p1, p2, p3 = thirds(coords)
-        s1, s2, s3 = thirds(square)
-
-        def with_square(part, square_part):
-            return jnp.where(row_w == 4, square_part, part + ones)
-
-        right_ref[column] = jnp.concatenate(
-            [with_square(p1, s1), with_square(p2, s2), with_square(p1, s3), p3, p2, p1], axis=0
-        ).astype(BF16)
-        moments = (coords + ones) * block[3:4]
-        m1, m2, m3 = thirds(moments)
-        mom_ref[column] = jnp.concatenate([m1, m2, m3, jnp.zeros_like(m1)], axis=0).astype(BF16)
-        return carry
-
-    lax.fori_loop(0, 16, column_step, 0)
-
-    row_c = row_iota(8)
-
-    def left_step(cell, carry):
-        x, y, z, block = cell_rows(cell)
-        shift = jnp.where(
-            row_c == 0, (x - 1).astype(F32), jnp.where(row_c == 1, (y - 1).astype(F32), z.astype(F32) - 1.5)
-        )
-        coords = jnp.where(row_c < 3, SPLIT_RATE * (block + shift), 0.0)
-        square = jnp.sum(coords * coords, axis=0, keepdims=True)
-        ones = jnp.where(row_c == 4, 1.0, 0.0)
-        p1, p2, p3 = thirds(-2.0 * coords)
-        s1, s2, s3 = thirds(square)
-
-        def with_square(part, square_part):
-            return jnp.where(row_c == 3, square_part, part + ones)
-
-        stacked = jnp.concatenate(
-            [with_square(p1, s1), with_square(p1, s2), with_square(p2, s3), p1, p2, p3, jnp.zeros((80, 128), F32)], axis=0
-        )
-        left_ref[cell] = jnp.transpose(stacked).astype(BF16)
-        return carry
-
-    grouped(6, left_step, 0)
-
-    def pair_step(cell, carry):
-        x, y, z, block = cell_rows(cell)
-        left = left_ref[cell][:, 0:48]
-
-        moments = jnp.zeros((128, 32), F32)
-        lanes = pl.ds(pl.multiple_of(z * 128, 128), 384)
-        for side in range(9):
-            column = (x + side // 3) * 4 + y + side % 3
-            square = dot(left, right_ref[column, :, lanes])
-            inverse = lax.rsqrt(square)
-            far = 1.0 - lax.erf(square * inverse)
-            bell = jnp.exp2(square * (-math.log2(math.e)))
-            factor = (inverse * inverse) * (far * inverse + (2.0 / math.sqrt(math.pi)) * bell)
-            high = factor.astype(BF16)
-            low = (factor - high.astype(F32)).astype(BF16)
-            other = mom_ref[column, :, lanes]
-            moments = moments + dot_rows(jnp.concatenate([high, low], axis=1), jnp.concatenate([other, other], axis=1))
-        moments = jnp.transpose(moments)
-        moments = moments[0:8] + moments[8:16] + moments[16:24]
-        shift = jnp.where(
-            row_c == 0, (x - 1).astype(F32), jnp.where(row_c == 1, (y - 1).astype(F32), z.astype(F32) - 1.5)
-        )
-        coords = SPLIT_RATE * (block + shift)
-        force_ref[cell] = (SPLIT_RATE * SPLIT_RATE) * block[3:4] * (coords * moments[3:4] - moments)
-        return carry
-
-    lax.fori_loop(0, 4, pair_step, 0)
+    for column in RIM:
+        column_step(jnp.int32(column), 0)
+    sweep(OUTER_PLAN, 0, 3, False)
+
+    return_copies = []
+    for num, side in enumerate(AHEAD):
+        shift = jnp.where(row_c == 0, 2.0 * SPLIT_RATE * side[0], jnp.where(row_c == 1, 2.0 * SPLIT_RATE * side[1], 0.0))
+        for place, (x, y) in enumerate(INTO[num]):
+            for z in range(3):
+                moments = summed(back_ref[3 * (4 * x + y) + z])
+                return_out[num, place, :, 128 * z : 128 * (z + 1)] = (moments - shift * moments[3:4])[0:4]
+        count = len(INTO[num])
+        copy = pltpu.make_async_remote_copy(
+            src_ref=return_out.at[num, pl.ds(0, count)], dst_ref=return_buf.at[num, pl.ds(0, count)],
+            send_sem=return_send.at[num], recv_sem=return_recv.at[num], device_id=near_id(side), device_id_type=MESH,
+        )
+        copy.start()
+        return_copies.append(copy)
 
     for copy in relays:
         copy.wait_recv()
-    rows = lax.broadcasted_iota(jnp.int32, (64, 128), 0)
-    cols = lax.broadcasted_iota(jnp.int32, (64, 128), 1)
-    member = (rows // 8) % 4
-    to_space = ((outer_x + member // 2) % 2) * 2 * laps + lap * 2 + (core + member % 2) % 2
-    from_space = outer_x * 2 * laps + ((lap + cols // 8) % laps) * 2 + core
-    total_x = 4 * spaces
-    dist = (4 * (to_space - from_space) + rows % 8 - cols % 8 + 2 * total_x) % total_x
-    dist = jnp.minimum(dist, total_x - dist).astype(F32)
-    wide = [2.0 * (total_x / fraction) ** 2 for fraction in COARSE_FRACTIONS]
-    bells = jnp.exp(-dist * dist * jnp.where(rows < 32, 1.0 / wide[0], 1.0 / wide[1]))
     gathered = jnp.concatenate([lap_buf[num] for num in range(laps)], axis=0)
-    along_x = lax.dot_general(
-        bells, gathered, (((1,), (0,)), ((), ())), precision=HIGHEST, preferred_element_type=F32
-    )
-    along_x = jnp.where(lax.broadcasted_iota(jnp.int32, (32, 128), 1) < 64, along_x[0:32], along_x[32:64])
-    parts = jnp.concatenate(halves(along_x), axis=0).astype(BF16)
+    along_x = dot(bells_ref[...], jnp.concatenate(halves(gathered), axis=1).astype(BF16))
+    along_x = along_x[0:128, 0:128] + along_x[0:128, 128:256] + along_x[128:256, 0:128]
+    turned = pltpu.roll(along_x, 64, 1)
+    along_x = jnp.where(lane < 64, along_x[0:32] + turned[64:96], turned[32:64] + along_x[96:128])
+    parts = jnp.concatenate(halves(jnp.concatenate([along_x[0:16], along_x[16:32]], axis=1)), axis=0).astype(BF16)
     shares = dot(parts, far_hi[...])
-    shares = shares[0:32] + shares[32:64] + dot(parts[0:32], far_lo[...])
+    shares = shares[0:16] + shares[16:32] + dot(parts[0:16], far_lo[...])
     for member_num in range(4):
         for step in range(subs):
-            plane_out[member_num * subs + step] = shares[8 * member_num : 8 * member_num + 8, 128 * step : 128 * (step + 1)]
+            plane_out[member_num * subs + step] = shares[4 * member_num : 4 * member_num + 4, 128 * step : 128 * (step + 1)]
     plane_copies = []
     for member_num, step in members:
         num = member_num * subs + step
@@ -438,7 +530,8 @@
         copy.start()
         plane_copies.append(copy)
 
-    lax.fori_loop(4, CELLS, pair_step, 0)
+    sweep(INNER_PLAN, 2, 3, False)
+    grouped(6, tables_step, 0)
 
     for copy in fine_copies:
         copy.wait_recv()
@@ -466,11 +559,17 @@
 
     fine_forces = [interpolate(cell, cell // 6, (cell // 3) % 2) for cell in range(CELLS)]
 
+    for copy in return_copies:
+        copy.wait_recv()
+    for cell in range(CELLS):
+        finish(cell)
+
     for copy in plane_copies:
         copy.wait_recv()
     window = plane_out[0]
     for member_num, step in members:
         window = window + plane_buf[member_num * subs + step]
+    window = jnp.concatenate([window, pltpu.roll(window, 64, 1)], axis=0)
     parts = jnp.concatenate(halves(window), axis=0).astype(BF16)[:, 0:48]
     for cell in range(CELLS):
         x, y, z = cell // 6, (cell // 3) % 2, cell % 3
@@ -483,7 +582,7 @@
             far = fine_forces[cell][k] + spread[:, 128 * k : 128 * (k + 1)]
             out_ref[k, x, z, pl.ds(y, 1), :] = force_ref[cell, pl.ds(k, 1), :] - 4.0 * charge * far
 
-    for copy in lap_copies + halo_copies + fine_copies + relays + plane_copies:
+    for copy in lap_copies + halo_copies + fine_copies + relays + return_copies + plane_copies:
         copy.wait_send()
 
 
@@ -500,20 +599,24 @@
         charges = jnp.transpose(charges, (0, 2, 1, 3))
         forces = pl.pallas_call(
             functools.partial(kernel, spaces, subs),
-            out_shape=jax.ShapeDtypeStruct(positions.shape, F32),
-            in_specs=[vmem_spec, vmem_spec, pl.BlockSpec(memory_space=pltpu.SMEM), any_spec, any_spec, any_spec, vmem_spec, any_spec, any_spec, any_spec],
+            out_shape=pltpu.VMEM(positions.shape, F32),
+            in_specs=[any_spec] * 10,
             out_specs=vmem_spec,
             scratch_shapes=[
+                pltpu.VMEM((3, 2, 3, 2, 128), F32),
+                pltpu.VMEM((2, 3, 2, 128), F32),
+                pltpu.SMEM((2, 2, 3), jnp.int32),
+                pltpu.VMEM((32, 16), F32),
                 pltpu.VMEM((512, 128), BF16),
                 pltpu.VMEM((256, 1152), BF16),
                 pltpu.VMEM((256, 1152), BF16),
                 pltpu.VMEM((192, 128), BF16),
-                pltpu.VMEM((128, 128 * subs), BF16),
-                pltpu.VMEM((128, 128 * subs), BF16),
-                pltpu.VMEM((4, 4, 8, 384), F32),
-                pltpu.VMEM((laps, 8, 128), F32),
-                pltpu.VMEM((planes, 8, 128), F32),
-                pltpu.VMEM((planes, 8, 128), F32),
+                pltpu.VMEM((256, 128 * subs), BF16),
+                pltpu.VMEM((256, 128 * subs), BF16),
+                pltpu.VMEM((4, 4, 4, 384), F32),
+                pltpu.VMEM((laps, 4, 128), F32),
+                pltpu.VMEM((planes, 4, 128), F32),
+                pltpu.VMEM((planes, 4, 128), F32),
                 pltpu.VMEM((9, 16, 128), F32),
                 pltpu.VMEM((8, 16, 128), F32),
                 pltpu.VMEM((4, 32, 128), F32),
@@ -522,17 +625,27 @@
                 pltpu.VMEM((48, CELLS * 384), BF16),
                 pltpu.VMEM((48, CELLS * 384), BF16),
                 pltpu.VMEM((8, CELLS * 384), F32),
-                pltpu.VMEM((CELLS, 128, 128), BF16),
+                pltpu.VMEM((256, 64), BF16),
+                pltpu.VMEM((CELLS, 256, 128), BF16),
                 pltpu.VMEM((16, 48, 640), BF16),
                 pltpu.VMEM((16, 32, 640), BF16),
+                pltpu.VMEM((2, 128, 3840), F32),
+                pltpu.VMEM((2, 128, 3840), F32),
+                pltpu.VMEM((CELLS, 128, 32), F32),
+                pltpu.VMEM((48, 32, 128), F32),
+                pltpu.VMEM((5, 2, 4, 384), F32),
+                pltpu.VMEM((5, 2, 4, 384), F32),
                 pltpu.VMEM((CELLS, 8, 128), F32),
-                pltpu.SemaphoreType.DMA((6,)),
-                pltpu.SemaphoreType.DMA((8,)),
-                pltpu.SemaphoreType.DMA((8,)),
+                pltpu.SemaphoreType.DMA((3,)),
+                pltpu.SemaphoreType.DMA((7,)),
+                pltpu.SemaphoreType.DMA((5,)),
+                pltpu.SemaphoreType.DMA((5,)),
                 pltpu.SemaphoreType.DMA((8,)),
                 pltpu.SemaphoreType.DMA((8,)),
                 pltpu.SemaphoreType.DMA((2,)),
                 pltpu.SemaphoreType.DMA((2,)),
+                pltpu.SemaphoreType.DMA((5,)),
+                pltpu.SemaphoreType.DMA((5,)),
                 pltpu.SemaphoreType.DMA((8,)),
                 pltpu.SemaphoreType.DMA((8,)),
                 pltpu.SemaphoreType.DMA((planes,)),

time: 46 us -> 33.1 us (0.72)
  Pallas kernels: 44.5 us -> 32.3 us
  local copies, waits for them, and re-layouts: 1.33 us -> 0.61 us
    pallas_call x1, Pallas kernels: 44.5 us -> 32.3 us  [body(): pl.pallas_call(functools.partial(kernel, spaces, subs), out_shape=pltpu.V...]
    unnamed x1, local copies, waits for them, and re-layouts: 1.33 us -> 0.61 us
where the time goes in v4:
time: 33.1 us; the launch traced here: 33 us
  Pallas kernels  32.3 us (98%)
  local copies, waits for them, and re-layouts  0.61 us (2%)
    pallas_call x1, Pallas kernels, body(): pl.pallas_call(functools.partial(kernel, spaces, subs), out_shape=pltpu.V...  32.3 us

profile of v4, /device:TPU:1, one launch (start us, length us, event | category | flops | bytes accessed | tf_op | source)
XLA Modules:
  0.0 33.0 jit_solution(8704806796497936425)
XLA Ops:
  0.0 32.3 %shard_map.100 = f32[3,2,3,2,128]{4,3,2,1,0:T(2,128)S(1)} custom-call(f32[3,2,3,2,128]{4,3,2,1,0:T(2,128)} %bitcast.4, f32[2,3,2,128]{3,2,1,0:T(2,128)} %bitcast.5, s32[2,2,3]{2,1,0:T(2,128)} %count_hbm.1, bf16[512,128]{1,0:T(8,128)(2,1)} %constant.14.clone.place_hbm, bf16[256,1152]{1,0:T(8,128)(2,1)} %constant.15.clone.wide_hi_hbm, ...), custom_call_target="tpu_custom_call" | custom-call | tf_op jit(solution)/shard_map/pallas_call | solution.py:600
  32.4 0.6 %copy.12 = f32[3,2,2,3,128]{4,2,3,1,0:T(2,128)} copy(f32[3,2,2,3,128]{4,2,3,1,0:T(2,128)S(1)} %bitcast.3) | data formatting | bytes 36864

commit v5 on v4

--- a/solution.py
+++ b/solution.py
@@ -156,7 +156,7 @@
     out_ref,
     pos_ref, charge_ref, count_ref, ring_ref, place_ref, wide_hi, wide_lo, select_ref, far_hi, far_lo,
     ext, lap_buf, plane_out, plane_buf, fine_out, fine_buf,
-    fine_sum, by_ref, wz_ref, pair_hi, pair_lo, vx_ref, bells_ref, left_ref, right_ref, mom_ref, square_ref, bell_ref, raw_ref, back_ref, return_out, return_buf, force_ref,
+    fine_sum, by_ref, wz_ref, pair_hi, pair_lo, vx_ref, bells_ref, left_ref, right_ref, mom_ref, square_ref, raw_ref, back_ref, return_out, return_buf, force_ref,
     input_sem, const_sem, halo_send, halo_recv, lap_send, lap_recv, relay_send, relay_recv, return_send, return_recv, fine_send, fine_recv, plane_send, plane_recv,
 ):
     laps = spaces // 4
@@ -194,12 +194,12 @@
 
     members = [(member, step) for member in range(4) for step in range(subs) if (member, step) != (0, 0)]
     barrier = pltpu.get_barrier_semaphore()
+    for step in sorted(LAPS, key=abs, reverse=True):
+        pl.semaphore_signal(barrier, inc=1, device_id=lap_id(step), device_id_type=MESH)
+    for member, step in sorted(members, key=lambda one: min(one[1], subs - one[1]), reverse=True):
+        pl.semaphore_signal(barrier, inc=1, device_id=plane_id(member, step), device_id_type=MESH)
     for side in NEAR:
         pl.semaphore_signal(barrier, inc=1, device_id=near_id(side), device_id_type=MESH)
-    for step in LAPS:
-        pl.semaphore_signal(barrier, inc=1, device_id=lap_id(step), device_id_type=MESH)
-    for member, step in members:
-        pl.semaphore_signal(barrier, inc=1, device_id=plane_id(member, step), device_id_type=MESH)
 
     for load in loads:
         load.start()
@@ -243,15 +243,15 @@
         return vx, vy, vz, block[3:4]
 
     pad = jnp.zeros((16, 128), F32)
-    total = jnp.zeros((16, 256), F32)
+    total = jnp.zeros((16, 128), F32)
     for cell in range(CELLS):
         vx, vy, vz, charge = coarse_weights(cell, spline)
         vz = vz * charge
         high, low = halves(jnp.concatenate([vz[k : k + 1] * vy for k in range(6)], axis=0))
-        right = jnp.concatenate([high, pad, high, pad, low, pad, low, pad], axis=0).astype(BF16)
+        right = jnp.concatenate([high, pad, low, pad], axis=0).astype(BF16)
         total = total + dot_rows(jnp.concatenate(halves(vx), axis=0).astype(BF16), right)
     total = total[0:8] + total[8:16]
-    total = total[:, 0:128] + total[:, 128:256]
+    total = total + pltpu.roll(total, 64, 1)
     lap_buf[0] = jnp.where(lane < 64, total[0:4], total[4:8])
 
     def tables_step(cell, carry):
@@ -271,29 +271,6 @@
         vx_ref[:, lanes] = jnp.concatenate([sx, vx, vx], axis=1)
         return carry
 
-    pl.semaphore_wait(barrier, len(NEAR) + len(LAPS) + len(members))
-
-    lap_copies = []
-    for num, step in enumerate(LAPS):
-        copy = pltpu.make_async_remote_copy(
-            src_ref=lap_buf.at[0], dst_ref=lap_buf.at[(-step) % laps], send_sem=lap_send.at[num], recv_sem=lap_recv.at[num],
-            device_id=lap_id(step), device_id_type=MESH,
-        )
-        copy.start()
-        lap_copies.append(copy)
-
-    halo_copies = []
-    for num, side in enumerate(AHEAD):
-        (x, y), (to_x, to_y) = FROM[num][0], INTO[num][0]
-        span_x, span_y = FROM[num][-1][0] - x + 1, FROM[num][-1][1] - y + 1
-        copy = pltpu.make_async_remote_copy(
-            src_ref=ext.at[pl.ds(x, span_x), pl.ds(y, span_y)], dst_ref=ext.at[pl.ds(to_x, span_x), pl.ds(to_y, span_y)],
-            send_sem=halo_send.at[num], recv_sem=halo_recv.at[num],
-            device_id=near_id((-side[0], -side[1])), device_id_type=MESH,
-        )
-        copy.start()
-        halo_copies.append(copy)
-
     row_w = row_iota(8, 640)
     slot_w = lax.broadcasted_iota(jnp.int32, (8, 640), 1) // 128
 
@@ -309,10 +286,9 @@
         ones = jnp.where(row_w == 3, 1.0, 0.0)
         p1, p2, p3 = thirds(coords)
         squares_of = thirds(square)
-        bells_of = thirds(-LOG2E * square)
 
         def with_square(part, num):
-            return jnp.where(row_w == 4, squares_of[num], jnp.where(row_w == 5, bells_of[num], part + ones))
+            return jnp.where(row_w == 4, squares_of[num], part + ones)
 
         right_ref[column] = jnp.concatenate(
             [with_square(p1, 0), with_square(p2, 1), with_square(p1, 2), p3, p2, p1], axis=0
@@ -331,23 +307,20 @@
         x, y, z, block = cell_rows(cell)
         block = padded(block)
         shift = jnp.where(
-            row_c == 0, (x - 1).astype(F32), jnp.where(row_c == 1, (y - 1).astype(F32), z.astype(F32) - 1.5)
+            row_c == 0, real(x - 1), jnp.where(row_c == 1, real(y - 1), real(z) - 1.5)
         )
         coords = jnp.where(row_c < 3, SPLIT_RATE * (block + shift), 0.0)
         square = jnp.sum(coords * coords, axis=0, keepdims=True)
 
-        def features(cross, own, ones_row):
-            ones = jnp.where(row_c == ones_row, 1.0, 0.0)
-            p1, p2, p3 = thirds(cross)
-            q1, q2, q3 = [jnp.where(row_c == 3, part, ones) for part in thirds(own)]
-            return jnp.concatenate([p1 + q1, p1 + q2, p2 + q3, p1, p2, p3, jnp.zeros((80, 128), F32)], axis=0)
-
-        left_ref[cell, 0:128, :] = jnp.transpose(features(-2.0 * coords, square, 4)).astype(BF16)
-        bell_own = math.log2(2.0 / math.sqrt(math.pi)) - LOG2E * square
-        left_ref[cell, 128:256, :] = jnp.transpose(features((2.0 * LOG2E) * coords, bell_own, 5)).astype(BF16)
+        ones = jnp.where(row_c == 4, 1.0, 0.0)
+        p1, p2, p3 = thirds(-2.0 * coords)
+        q1, q2, q3 = [jnp.where(row_c == 3, part, ones) for part in thirds(square)]
+        stacked = jnp.concatenate([p1 + q1, p1 + q2, p2 + q3, p1, p2, p3, jnp.zeros((80, 128), F32)], axis=0)
+        left_ref[cell] = jnp.transpose(stacked).astype(BF16)
         return carry
 
-    grouped(6, left_step, 0)
+    for cell in range(CELLS):
+        left_step(cell, 0)
 
     def slot_lanes(slot, count=1):
         return pl.ds(pl.multiple_of(slot * 128, 128), 128 * count)
@@ -357,10 +330,9 @@
         for one in range(4):
             left = left_ref[3 * one + z][:, 0:48]
             for column, slots in plan[one]:
-                both = dot(left, right_ref[column, :, slot_lanes(z + slots[0], len(slots))])
-                lanes = slice(128 * at, 128 * (at + len(slots)))
-                square_ref[half, :, lanes] = both[0:128]
-                bell_ref[half, :, lanes] = both[128:256]
+                square_ref[half, :, 128 * at : 128 * (at + len(slots))] = dot(
+                    left, right_ref[column, :, slot_lanes(z + slots[0], len(slots))]
+                )
                 at += len(slots)
 
     def pulls(plan, z, half, first):
@@ -372,7 +344,8 @@
                 square = square_ref[half, :, 128 * at : 128 * (at + 1)]
                 inverse = lax.rsqrt(square)
                 far = 1.0 - lax.erf(square * inverse)
-                factor = (inverse * inverse) * (far * inverse + jnp.exp2(bell_ref[half, :, 128 * at : 128 * (at + 1)]))
+                bell = (2.0 / math.sqrt(math.pi)) * jnp.exp2(square * -LOG2E)
+                factor = (inverse * inverse) * (far * inverse + bell)
                 high = factor.astype(BF16)
                 low = (factor - high.astype(F32)).astype(BF16)
                 other = mom_ref[column, :, slot_lanes(z + slot)]
@@ -408,18 +381,13 @@
         coords = SPLIT_RATE * (block + shift)
         force_ref[cell] = (SPLIT_RATE * SPLIT_RATE) * block[3:4] * (coords * moments[3:4] - moments)
 
-    back_ref[...] = jnp.zeros_like(back_ref)
-    for one in range(4):
-        raw_ref[3 * one + 2] = jnp.zeros((128, 32), F32)
-    sweep(INNER_PLAN, 0, 2, True)
-
     fine_sum[...] = jnp.zeros_like(fine_sum)
 
     def fine_step(cell, carry):
         x, y, z, block = cell_rows(cell)
         at_x = 4.0 * block[0:1] - (row8 - 1.0)
         at_y = 4.0 * block[1:2] - (row8 - 1.0)
-        at_z = wrapped(4.0 * block[2:3] + (4 * z).astype(F32) - row16)
+        at_z = wrapped(4.0 * block[2:3] + real(4 * z) - row16)
         bx, by = spline(at_x), spline(at_y)
         bz = jnp.where(row16 < 12.0, spline(at_z), 0.0)
         sz = jnp.where(row16 < 12.0, spline_slope(at_z), 0.0)
@@ -433,7 +401,8 @@
         fine_sum[cell // 3] += dot_rows(left, right)
         return carry
 
-    grouped(6, fine_step, 0)
+    for cell in range(CELLS):
+        fine_step(cell, 0)
     for load in loads:
         load.wait()
     boxes = jnp.concatenate([fine_sum[num, 0:16] + fine_sum[num, 16:32] for num in range(4)], axis=1)
@@ -448,16 +417,6 @@
     fine_all = fine_all[0:16] + fine_all[16:32] + dot(parts[0:16], wide_lo[...])
     for num in range(9):
         fine_out[num] = fine_all[:, 128 * num : 128 * (num + 1)]
-    fine_copies = []
-    for num, side in enumerate(NEAR):
-        copy = pltpu.make_async_remote_copy(
-            src_ref=fine_out.at[SIDES.index(side)], dst_ref=fine_buf.at[num],
-            send_sem=fine_send.at[num], recv_sem=fine_recv.at[num], device_id=near_id(side), device_id_type=MESH,
-        )
-        copy.start()
-        fine_copies.append(copy)
-
-
     rows = lax.broadcasted_iota(jnp.int32, (128, 64), 0)
     cols = lax.broadcasted_iota(jnp.int32, (128, 64), 1)
     member = (rows // 4) % 4
@@ -472,8 +431,46 @@
     bells = jnp.exp(-dist * dist * jnp.where((rows // 32) % 2 == 0, 1.0 / wide[0], 1.0 / wide[1]))
     bells_ref[...] = jnp.concatenate(halves(bells), axis=0).astype(BF16)
 
-    for copy in lap_copies:
-        copy.wait_recv()
+    back_ref[...] = jnp.zeros_like(back_ref)
+    for one in range(4):
+        raw_ref[3 * one + 2] = jnp.zeros((128, 32), F32)
+
+    pl.semaphore_wait(barrier, len(NEAR) + len(LAPS) + len(members))
+
+    for num, step in enumerate(LAPS):
+        copy = pltpu.make_async_remote_copy(
+            src_ref=lap_buf.at[0], dst_ref=lap_buf.at[(-step) % laps], send_sem=lap_send.at[0], recv_sem=lap_recv.at[num // 4],
+            device_id=lap_id(step), device_id_type=MESH,
+        )
+        copy.start()
+
+    halo_copies = []
+    for num, side in enumerate(AHEAD):
+        (x, y), (to_x, to_y) = FROM[num][0], INTO[num][0]
+        span_x, span_y = FROM[num][-1][0] - x + 1, FROM[num][-1][1] - y + 1
+        copy = pltpu.make_async_remote_copy(
+            src_ref=ext.at[pl.ds(x, span_x), pl.ds(y, span_y)], dst_ref=ext.at[pl.ds(to_x, span_x), pl.ds(to_y, span_y)],
+            send_sem=halo_send.at[num], recv_sem=halo_recv.at[num],
+            device_id=near_id((-side[0], -side[1])), device_id_type=MESH,
+        )
+        copy.start()
+        halo_copies.append(copy)
+
+    for num, side in enumerate(NEAR):
+        copy = pltpu.make_async_remote_copy(
+            src_ref=fine_out.at[SIDES.index(side)], dst_ref=fine_buf.at[num],
+            send_sem=fine_send.at[0], recv_sem=fine_recv.at[0], device_id=near_id(side), device_id_type=MESH,
+        )
+        copy.start()
+
+
+    sweep(INNER_PLAN, 0, 2, True)
+
+    for num, start in enumerate((laps - 4, 1)):
+        pltpu.make_async_remote_copy(
+            src_ref=lap_buf.at[pl.ds(start, 4)], dst_ref=lap_buf.at[pl.ds(start, 4)], send_sem=lap_send.at[0], recv_sem=lap_recv.at[num],
+            device_id=lap_id(1), device_id_type=MESH,
+        ).wait_recv()
     relays = []
     for num, (src, dst, step) in enumerate((
         (pl.ds(1, 4), pl.ds(5, 4), -4),
@@ -520,21 +517,22 @@
     for member_num in range(4):
         for step in range(subs):
             plane_out[member_num * subs + step] = shares[4 * member_num : 4 * member_num + 4, 128 * step : 128 * (step + 1)]
-    plane_copies = []
     for member_num, step in members:
         num = member_num * subs + step
         copy = pltpu.make_async_remote_copy(
-            src_ref=plane_out.at[num], dst_ref=plane_buf.at[num], send_sem=plane_send.at[num], recv_sem=plane_recv.at[num],
+            src_ref=plane_out.at[num], dst_ref=plane_buf.at[num], send_sem=plane_send.at[0], recv_sem=plane_recv.at[0],
             device_id=plane_id(member_num, step), device_id_type=MESH,
         )
         copy.start()
-        plane_copies.append(copy)
+
 
     sweep(INNER_PLAN, 2, 3, False)
     grouped(6, tables_step, 0)
 
-    for copy in fine_copies:
-        copy.wait_recv()
+    fine_all_in = pltpu.make_async_remote_copy(
+        src_ref=fine_buf, dst_ref=fine_buf, send_sem=fine_send.at[0], recv_sem=fine_recv.at[0], device_id=near_id((0, 1)), device_id_type=MESH,
+    )
+    fine_all_in.wait_recv()
     fine = fine_out[SIDES.index((0, 0))]
     for num in range(8):
         fine = fine + fine_buf[num]
@@ -564,8 +562,10 @@
     for cell in range(CELLS):
         finish(cell)
 
-    for copy in plane_copies:
-        copy.wait_recv()
+    plane_all_in = pltpu.make_async_remote_copy(
+        src_ref=plane_out.at[pl.ds(1, 4 * subs - 1)], dst_ref=plane_buf.at[pl.ds(1, 4 * subs - 1)], send_sem=plane_send.at[0], recv_sem=plane_recv.at[0], device_id=plane_id(0, 1), device_id_type=MESH,
+    )
+    plane_all_in.wait_recv()
     window = plane_out[0]
     for member_num, step in members:
         window = window + plane_buf[member_num * subs + step]
@@ -582,7 +582,13 @@
             far = fine_forces[cell][k] + spread[:, 128 * k : 128 * (k + 1)]
             out_ref[k, x, z, pl.ds(y, 1), :] = force_ref[cell, pl.ds(k, 1), :] - 4.0 * charge * far
 
-    for copy in lap_copies + halo_copies + fine_copies + relays + return_copies + plane_copies:
+    lap_all_out = pltpu.make_async_remote_copy(
+        src_ref=lap_buf.at[pl.ds(0, 8)], dst_ref=lap_buf.at[pl.ds(0, 8)], send_sem=lap_send.at[0], recv_sem=lap_recv.at[0], device_id=lap_id(1), device_id_type=MESH,
+    )
+    lap_all_out.wait_send()
+    fine_all_in.wait_send()
+    plane_all_in.wait_send()
+    for copy in halo_copies + relays + return_copies:
         copy.wait_send()
 
 
@@ -626,10 +632,9 @@
                 pltpu.VMEM((48, CELLS * 384), BF16),
                 pltpu.VMEM((8, CELLS * 384), F32),
                 pltpu.VMEM((256, 64), BF16),
-                pltpu.VMEM((CELLS, 256, 128), BF16),
+                pltpu.VMEM((CELLS, 128, 128), BF16),
                 pltpu.VMEM((16, 48, 640), BF16),
                 pltpu.VMEM((16, 32, 640), BF16),
-                pltpu.VMEM((2, 128, 3840), F32),
                 pltpu.VMEM((2, 128, 3840), F32),
                 pltpu.VMEM((CELLS, 128, 32), F32),
                 pltpu.VMEM((48, 32, 128), F32),
@@ -640,16 +645,16 @@
                 pltpu.SemaphoreType.DMA((7,)),
                 pltpu.SemaphoreType.DMA((5,)),
                 pltpu.SemaphoreType.DMA((5,)),
-                pltpu.SemaphoreType.DMA((8,)),
-                pltpu.SemaphoreType.DMA((8,)),
+                pltpu.SemaphoreType.DMA((1,)),
+                pltpu.SemaphoreType.DMA((2,)),
                 pltpu.SemaphoreType.DMA((2,)),
                 pltpu.SemaphoreType.DMA((2,)),
                 pltpu.SemaphoreType.DMA((5,)),
                 pltpu.SemaphoreType.DMA((5,)),
-                pltpu.SemaphoreType.DMA((8,)),
-                pltpu.SemaphoreType.DMA((8,)),
-                pltpu.SemaphoreType.DMA((planes,)),
-                pltpu.SemaphoreType.DMA((planes,)),
+                pltpu.SemaphoreType.DMA((1,)),
+                pltpu.SemaphoreType.DMA((1,)),
+                pltpu.SemaphoreType.DMA((1,)),
+                pltpu.SemaphoreType.DMA((1,)),
             ],
             compiler_params=pltpu.CompilerParams(collective_id=0, has_side_effects=True),
         )(

time: 33.1 us -> 32 us (0.967)
  Pallas kernels: 32.3 us -> 31.2 us
    pallas_call x1, Pallas kernels: 32.3 us -> 31.2 us  [body(): pl.pallas_call(functools.partial(kernel, spaces, subs), out_shape=pltpu.V...]
where the time goes in v5:
time: 32 us; the launch traced here: 31.8 us
  Pallas kernels  31.2 us (98%)
  local copies, waits for them, and re-layouts  0.61 us (2%)
    pallas_call x1, Pallas kernels, body(): pl.pallas_call(functools.partial(kernel, spaces, subs), out_shape=pltpu.V...  31.2 us

profile of v5, /device:TPU:1, one launch (start us, length us, event | category | flops | bytes accessed | tf_op | source)
XLA Modules:
  0.0 31.8 jit_solution(6279944373657072425)
XLA Ops:
  0.0 31.2 %shard_map.100 = f32[3,2,3,2,128]{4,3,2,1,0:T(2,128)S(1)} custom-call(f32[3,2,3,2,128]{4,3,2,1,0:T(2,128)} %bitcast.4, f32[2,3,2,128]{3,2,1,0:T(2,128)} %bitcast.5, s32[2,2,3]{2,1,0:T(2,128)} %count_hbm.1, bf16[512,128]{1,0:T(8,128)(2,1)} %constant.14.clone.place_hbm, bf16[256,1152]{1,0:T(8,128)(2,1)} %constant.15.clone.wide_hi_hbm, ...), custom_call_target="tpu_custom_call" | custom-call | tf_op jit(solution)/shard_map/pallas_call | solution.py:606
  31.2 0.6 %copy.12 = f32[3,2,2,3,128]{4,2,3,1,0:T(2,128)} copy(f32[3,2,2,3,128]{4,2,3,1,0:T(2,128)S(1)} %bitcast.3) | data formatting | bytes 36864

commit v6 on v5

--- a/solution.py
+++ b/solution.py
@@ -156,7 +156,7 @@
     out_ref,
     pos_ref, charge_ref, count_ref, ring_ref, place_ref, wide_hi, wide_lo, select_ref, far_hi, far_lo,
     ext, lap_buf, plane_out, plane_buf, fine_out, fine_buf,
-    fine_sum, by_ref, wz_ref, pair_hi, pair_lo, vx_ref, bells_ref, left_ref, right_ref, mom_ref, square_ref, raw_ref, back_ref, return_out, return_buf, force_ref,
+    fine_sum, by_ref, wz_ref, pair_hi, pair_lo, vx_ref, bells_ref, left_ref, right_ref, mom_ref, square_ref, raw_ref, back_ref, return_out, return_buf, seven_ref, force_ref,
     input_sem, const_sem, halo_send, halo_recv, lap_send, lap_recv, relay_send, relay_recv, return_send, return_recv, fine_send, fine_recv, plane_send, plane_recv,
 ):
     laps = spaces // 4
@@ -381,6 +381,43 @@
         coords = SPLIT_RATE * (block + shift)
         force_ref[cell] = (SPLIT_RATE * SPLIT_RATE) * block[3:4] * (coords * moments[3:4] - moments)
 
+    rows = lax.broadcasted_iota(jnp.int32, (128, 64), 0)
+    cols = lax.broadcasted_iota(jnp.int32, (128, 64), 1)
+    member = (rows // 4) % 4
+    to_space = ((outer_x + member // 2) % 2) * 2 * laps + lap * 2 + (core + member % 2) % 2
+    from_space = outer_x * 2 * laps + ((lap + cols // 4) % laps) * 2 + core
+    total_x = 4 * spaces
+    to_row = 3 * ((rows // 16) % 2) + rows % 4
+    from_row = 3 * (rows // 64) + cols % 4
+    dist = (4 * (to_space - from_space) + to_row - from_row + 2 * total_x) % total_x
+    dist = jnp.minimum(dist, total_x - dist).astype(F32)
+    wide = [2.0 * (total_x / fraction) ** 2 for fraction in COARSE_FRACTIONS]
+    bells = jnp.exp(-dist * dist * jnp.where((rows // 32) % 2 == 0, 1.0 / wide[0], 1.0 / wide[1]))
+    bells_ref[...] = jnp.concatenate(halves(bells), axis=0).astype(BF16)
+
+    back_ref[...] = jnp.zeros_like(back_ref)
+    for one in range(4):
+        raw_ref[3 * one + 2] = jnp.zeros((128, 32), F32)
+
+    pl.semaphore_wait(barrier, len(NEAR) + len(LAPS) + len(members))
+
+    for num, step in sorted(enumerate(LAPS), key=lambda one: -abs(one[1])):
+        copy = pltpu.make_async_remote_copy(
+            src_ref=lap_buf.at[0], dst_ref=lap_buf.at[(-step) % laps], send_sem=lap_send.at[0], recv_sem=lap_recv.at[num // 4],
+            device_id=lap_id(step), device_id_type=MESH,
+        )
+        copy.start()
+
+    for num, side in enumerate(AHEAD):
+        (x, y), (to_x, to_y) = FROM[num][0], INTO[num][0]
+        span_x, span_y = FROM[num][-1][0] - x + 1, FROM[num][-1][1] - y + 1
+        copy = pltpu.make_async_remote_copy(
+            src_ref=ext.at[pl.ds(x, span_x), pl.ds(y, span_y)], dst_ref=ext.at[pl.ds(to_x, span_x), pl.ds(to_y, span_y)],
+            send_sem=halo_send.at[0], recv_sem=halo_recv.at[0],
+            device_id=near_id((-side[0], -side[1])), device_id_type=MESH,
+        )
+        copy.start()
+
     fine_sum[...] = jnp.zeros_like(fine_sum)
 
     def fine_step(cell, carry):
@@ -417,45 +454,6 @@
     fine_all = fine_all[0:16] + fine_all[16:32] + dot(parts[0:16], wide_lo[...])
     for num in range(9):
         fine_out[num] = fine_all[:, 128 * num : 128 * (num + 1)]
-    rows = lax.broadcasted_iota(jnp.int32, (128, 64), 0)
-    cols = lax.broadcasted_iota(jnp.int32, (128, 64), 1)
-    member = (rows // 4) % 4
-    to_space = ((outer_x + member // 2) % 2) * 2 * laps + lap * 2 + (core + member % 2) % 2
-    from_space = outer_x * 2 * laps + ((lap + cols // 4) % laps) * 2 + core
-    total_x = 4 * spaces
-    to_row = 3 * ((rows // 16) % 2) + rows % 4
-    from_row = 3 * (rows // 64) + cols % 4
-    dist = (4 * (to_space - from_space) + to_row - from_row + 2 * total_x) % total_x
-    dist = jnp.minimum(dist, total_x - dist).astype(F32)
-    wide = [2.0 * (total_x / fraction) ** 2 for fraction in COARSE_FRACTIONS]
-    bells = jnp.exp(-dist * dist * jnp.where((rows // 32) % 2 == 0, 1.0 / wide[0], 1.0 / wide[1]))
-    bells_ref[...] = jnp.concatenate(halves(bells), axis=0).astype(BF16)
-
-    back_ref[...] = jnp.zeros_like(back_ref)
-    for one in range(4):
-        raw_ref[3 * one + 2] = jnp.zeros((128, 32), F32)
-
-    pl.semaphore_wait(barrier, len(NEAR) + len(LAPS) + len(members))
-
-    for num, step in enumerate(LAPS):
-        copy = pltpu.make_async_remote_copy(
-            src_ref=lap_buf.at[0], dst_ref=lap_buf.at[(-step) % laps], send_sem=lap_send.at[0], recv_sem=lap_recv.at[num // 4],
-            device_id=lap_id(step), device_id_type=MESH,
-        )
-        copy.start()
-
-    halo_copies = []
-    for num, side in enumerate(AHEAD):
-        (x, y), (to_x, to_y) = FROM[num][0], INTO[num][0]
-        span_x, span_y = FROM[num][-1][0] - x + 1, FROM[num][-1][1] - y + 1
-        copy = pltpu.make_async_remote_copy(
-            src_ref=ext.at[pl.ds(x, span_x), pl.ds(y, span_y)], dst_ref=ext.at[pl.ds(to_x, span_x), pl.ds(to_y, span_y)],
-            send_sem=halo_send.at[num], recv_sem=halo_recv.at[num],
-            device_id=near_id((-side[0], -side[1])), device_id_type=MESH,
-        )
-        copy.start()
-        halo_copies.append(copy)
-
     for num, side in enumerate(NEAR):
         copy = pltpu.make_async_remote_copy(
             src_ref=fine_out.at[SIDES.index(side)], dst_ref=fine_buf.at[num],
@@ -483,13 +481,15 @@
         copy.start()
         relays.append(copy)
 
-    for copy in halo_copies:
-        copy.wait_recv()
+    halo_all = pltpu.make_async_remote_copy(
+        src_ref=seven_ref, dst_ref=seven_ref, send_sem=halo_send.at[0], recv_sem=halo_recv.at[0],
+        device_id=near_id((0, 1)), device_id_type=MESH,
+    )
+    halo_all.wait_recv()
     for column in RIM:
         column_step(jnp.int32(column), 0)
     sweep(OUTER_PLAN, 0, 3, False)
 
-    return_copies = []
     for num, side in enumerate(AHEAD):
         shift = jnp.where(row_c == 0, 2.0 * SPLIT_RATE * side[0], jnp.where(row_c == 1, 2.0 * SPLIT_RATE * side[1], 0.0))
         for place, (x, y) in enumerate(INTO[num]):
@@ -499,10 +499,9 @@
         count = len(INTO[num])
         copy = pltpu.make_async_remote_copy(
             src_ref=return_out.at[num, pl.ds(0, count)], dst_ref=return_buf.at[num, pl.ds(0, count)],
-            send_sem=return_send.at[num], recv_sem=return_recv.at[num], device_id=near_id(side), device_id_type=MESH,
+            send_sem=return_send.at[0], recv_sem=return_recv.at[0], device_id=near_id(side), device_id_type=MESH,
         )
         copy.start()
-        return_copies.append(copy)
 
     for copy in relays:
         copy.wait_recv()
@@ -517,7 +516,7 @@
     for member_num in range(4):
         for step in range(subs):
             plane_out[member_num * subs + step] = shares[4 * member_num : 4 * member_num + 4, 128 * step : 128 * (step + 1)]
-    for member_num, step in members:
+    for member_num, step in sorted(members, key=lambda one: -min(one[1], subs - one[1])):
         num = member_num * subs + step
         copy = pltpu.make_async_remote_copy(
             src_ref=plane_out.at[num], dst_ref=plane_buf.at[num], send_sem=plane_send.at[0], recv_sem=plane_recv.at[0],
@@ -557,8 +556,11 @@
 
     fine_forces = [interpolate(cell, cell // 6, (cell // 3) % 2) for cell in range(CELLS)]
 
-    for copy in return_copies:
-        copy.wait_recv()
+    return_all = pltpu.make_async_remote_copy(
+        src_ref=seven_ref, dst_ref=seven_ref, send_sem=return_send.at[0], recv_sem=return_recv.at[0],
+        device_id=near_id((0, 1)), device_id_type=MESH,
+    )
+    return_all.wait_recv()
     for cell in range(CELLS):
         finish(cell)
 
@@ -566,9 +568,10 @@
         src_ref=plane_out.at[pl.ds(1, 4 * subs - 1)], dst_ref=plane_buf.at[pl.ds(1, 4 * subs - 1)], send_sem=plane_send.at[0], recv_sem=plane_recv.at[0], device_id=plane_id(0, 1), device_id_type=MESH,
     )
     plane_all_in.wait_recv()
-    window = plane_out[0]
-    for member_num, step in members:
-        window = window + plane_buf[member_num * subs + step]
+    pieces = [plane_out[0]] + [plane_buf[member_num * subs + step] for member_num, step in members]
+    while len(pieces) > 1:
+        pieces = [sum(pieces[num : num + 2][1:], pieces[num]) for num in range(0, len(pieces), 2)]
+    window = pieces[0]
     window = jnp.concatenate([window, pltpu.roll(window, 64, 1)], axis=0)
     parts = jnp.concatenate(halves(window), axis=0).astype(BF16)[:, 0:48]
     for cell in range(CELLS):
@@ -588,7 +591,9 @@
     lap_all_out.wait_send()
     fine_all_in.wait_send()
     plane_all_in.wait_send()
-    for copy in halo_copies + relays + return_copies:
+    halo_all.wait_send()
+    return_all.wait_send()
+    for copy in relays:
         copy.wait_send()
 
 
@@ -640,17 +645,18 @@
                 pltpu.VMEM((48, 32, 128), F32),
                 pltpu.VMEM((5, 2, 4, 384), F32),
                 pltpu.VMEM((5, 2, 4, 384), F32),
+                pltpu.VMEM((7, 4, 384), F32),
                 pltpu.VMEM((CELLS, 8, 128), F32),
                 pltpu.SemaphoreType.DMA((3,)),
                 pltpu.SemaphoreType.DMA((7,)),
-                pltpu.SemaphoreType.DMA((5,)),
-                pltpu.SemaphoreType.DMA((5,)),
+                pltpu.SemaphoreType.DMA((1,)),
+                pltpu.SemaphoreType.DMA((1,)),
                 pltpu.SemaphoreType.DMA((1,)),
                 pltpu.SemaphoreType.DMA((2,)),
                 pltpu.SemaphoreType.DMA((2,)),
                 pltpu.SemaphoreType.DMA((2,)),
-                pltpu.SemaphoreType.DMA((5,)),
-                pltpu.SemaphoreType.DMA((5,)),
+                pltpu.SemaphoreType.DMA((1,)),
+                pltpu.SemaphoreType.DMA((1,)),
                 pltpu.SemaphoreType.DMA((1,)),
                 pltpu.SemaphoreType.DMA((1,)),
                 pltpu.SemaphoreType.DMA((1,)),

time: 32 us -> 31.3 us (0.978)
  Pallas kernels: 31.2 us -> 30.6 us
    pallas_call x1, Pallas kernels: 31.2 us -> 30.6 us  [body(): pl.pallas_call(functools.partial(kernel, spaces, subs), out_shape=pltpu.V...]
where the time goes in v6:
time: 31.3 us; the launch traced here: 31.2 us
  Pallas kernels  30.6 us (98%)
  local copies, waits for them, and re-layouts  0.61 us (2%)
    pallas_call x1, Pallas kernels, body(): pl.pallas_call(functools.partial(kernel, spaces, subs), out_shape=pltpu.V...  30.6 us

profile of v6, /device:TPU:1, one launch (start us, length us, event | category | flops | bytes accessed | tf_op | source)
XLA Modules:
  0.0 31.2 jit_solution(16339014991959696215)
XLA Ops:
  0.0 30.6 %shard_map.100 = f32[3,2,3,2,128]{4,3,2,1,0:T(2,128)S(1)} custom-call(f32[3,2,3,2,128]{4,3,2,1,0:T(2,128)} %bitcast.4, f32[2,3,2,128]{3,2,1,0:T(2,128)} %bitcast.5, s32[2,2,3]{2,1,0:T(2,128)} %count_hbm.1, bf16[512,128]{1,0:T(8,128)(2,1)} %constant.14.clone.place_hbm, bf16[256,1152]{1,0:T(8,128)(2,1)} %constant.15.clone.wide_hi_hbm, ...), custom_call_target="tpu_custom_call" | custom-call | tf_op jit(solution)/shard_map/pallas_call | solution.py:611
  30.6 0.6 %copy.12 = f32[3,2,2,3,128]{4,2,3,1,0:T(2,128)} copy(f32[3,2,2,3,128]{4,2,3,1,0:T(2,128)S(1)} %bitcast.3) | data formatting | bytes 36864

commit v7 on v6

--- a/solution.py
+++ b/solution.py
@@ -268,7 +268,8 @@
         high, low = halves(tables)
         pair_hi[:, lanes] = high.astype(BF16)
         pair_lo[:, lanes] = low.astype(BF16)
-        vx_ref[:, lanes] = jnp.concatenate([sx, vx, vx], axis=1)
+        pull = -4.0 * charge
+        vx_ref[:, lanes] = jnp.concatenate([sx * pull, vx * pull, vx * pull], axis=1)
         return carry
 
     row_w = row_iota(8, 640)
@@ -464,16 +465,16 @@
 
     sweep(INNER_PLAN, 0, 2, True)
 
-    for num, start in enumerate((laps - 4, 1)):
-        pltpu.make_async_remote_copy(
-            src_ref=lap_buf.at[pl.ds(start, 4)], dst_ref=lap_buf.at[pl.ds(start, 4)], send_sem=lap_send.at[0], recv_sem=lap_recv.at[num],
-            device_id=lap_id(1), device_id_type=MESH,
-        ).wait_recv()
     relays = []
     for num, (src, dst, step) in enumerate((
         (pl.ds(1, 4), pl.ds(5, 4), -4),
         (pl.ds(laps - 3, 3), pl.ds(laps - 7, 3), 4),
     )):
+        landed = lap_buf.at[pl.ds(laps - 4 if num else 1, 4)]
+        pltpu.make_async_remote_copy(
+            src_ref=landed, dst_ref=landed, send_sem=lap_send.at[0], recv_sem=lap_recv.at[1 - num],
+            device_id=lap_id(1), device_id_type=MESH,
+        ).wait_recv()
         copy = pltpu.make_async_remote_copy(
             src_ref=lap_buf.at[src], dst_ref=lap_buf.at[dst], send_sem=relay_send.at[num], recv_sem=relay_recv.at[num],
             device_id=lap_id(step), device_id_type=MESH,
@@ -563,6 +564,10 @@
     return_all.wait_recv()
     for cell in range(CELLS):
         finish(cell)
+        x, y, z = cell // 6, (cell // 3) % 2, cell % 3
+        pull = -4.0 * ext[1 + x, 1 + y, pl.ds(3, 1), pl.ds(128 * z, 128)]
+        for k in range(3):
+            force_ref[cell, pl.ds(k, 1), :] += pull * fine_forces[cell][k]
 
     plane_all_in = pltpu.make_async_remote_copy(
         src_ref=plane_out.at[pl.ds(1, 4 * subs - 1)], dst_ref=plane_buf.at[pl.ds(1, 4 * subs - 1)], send_sem=plane_send.at[0], recv_sem=plane_recv.at[0], device_id=plane_id(0, 1), device_id_type=MESH,
@@ -580,10 +585,8 @@
         spread = dot(parts, pair_hi[:, lanes])
         spread = spread[0:8] + spread[8:16] + dot(parts, pair_lo[:, lanes])[0:8]
         spread = jnp.sum(spread * vx_ref[:, lanes], axis=0, keepdims=True)
-        charge = ext[1 + x, 1 + y, pl.ds(3, 1), pl.ds(128 * z, 128)]
         for k in range(3):
-            far = fine_forces[cell][k] + spread[:, 128 * k : 128 * (k + 1)]
-            out_ref[k, x, z, pl.ds(y, 1), :] = force_ref[cell, pl.ds(k, 1), :] - 4.0 * charge * far
+            out_ref[k, x, z, pl.ds(y, 1), :] = force_ref[cell, pl.ds(k, 1), :] + spread[:, 128 * k : 128 * (k + 1)]
 
     lap_all_out = pltpu.make_async_remote_copy(
         src_ref=lap_buf.at[pl.ds(0, 8)], dst_ref=lap_buf.at[pl.ds(0, 8)], send_sem=lap_send.at[0], recv_sem=lap_recv.at[0], device_id=lap_id(1), device_id_type=MESH,

time: 31.3 us -> 31.4 us (level)
  no operation moved by 1% of the time
where the time goes in v7:
time: 31.4 us; the launch traced here: 31.2 us
  Pallas kernels  30.6 us (97%)
  local copies, waits for them, and re-layouts  0.61 us (2%)
    pallas_call x1, Pallas kernels, body(): pl.pallas_call(functools.partial(kernel, spaces, subs), out_shape=pltpu.V...  30.6 us

profile of v7, /device:TPU:1, one launch (start us, length us, event | category | flops | bytes accessed | tf_op | source)
XLA Modules:
  0.0 31.2 jit_solution(9795792498999673139)
XLA Ops:
  0.0 30.6 %shard_map.100 = f32[3,2,3,2,128]{4,3,2,1,0:T(2,128)S(1)} custom-call(f32[3,2,3,2,128]{4,3,2,1,0:T(2,128)} %bitcast.4, f32[2,3,2,128]{3,2,1,0:T(2,128)} %bitcast.5, s32[2,2,3]{2,1,0:T(2,128)} %count_hbm.1, bf16[512,128]{1,0:T(8,128)(2,1)} %constant.14.clone.place_hbm, bf16[256,1152]{1,0:T(8,128)(2,1)} %constant.15.clone.wide_hi_hbm, ...), custom_call_target="tpu_custom_call" | custom-call | tf_op jit(solution)/shard_map/pallas_call | solution.py:614
  30.6 0.6 %copy.12 = f32[3,2,2,3,128]{4,2,3,1,0:T(2,128)} copy(f32[3,2,2,3,128]{4,2,3,1,0:T(2,128)S(1)} %bitcast.3) | data formatting | bytes 36864

commit v8 on v6

--- a/solution.py
+++ b/solution.py
@@ -464,16 +464,16 @@
 
     sweep(INNER_PLAN, 0, 2, True)
 
-    for num, start in enumerate((laps - 4, 1)):
-        pltpu.make_async_remote_copy(
-            src_ref=lap_buf.at[pl.ds(start, 4)], dst_ref=lap_buf.at[pl.ds(start, 4)], send_sem=lap_send.at[0], recv_sem=lap_recv.at[num],
-            device_id=lap_id(1), device_id_type=MESH,
-        ).wait_recv()
     relays = []
     for num, (src, dst, step) in enumerate((
         (pl.ds(1, 4), pl.ds(5, 4), -4),
         (pl.ds(laps - 3, 3), pl.ds(laps - 7, 3), 4),
     )):
+        landed = lap_buf.at[pl.ds(laps - 4 if num else 1, 4)]
+        pltpu.make_async_remote_copy(
+            src_ref=landed, dst_ref=landed, send_sem=lap_send.at[0], recv_sem=lap_recv.at[1 - num],
+            device_id=lap_id(1), device_id_type=MESH,
+        ).wait_recv()
         copy = pltpu.make_async_remote_copy(
             src_ref=lap_buf.at[src], dst_ref=lap_buf.at[dst], send_sem=relay_send.at[num], recv_sem=relay_recv.at[num],
             device_id=lap_id(step), device_id_type=MESH,

time: 31.3 us -> 31.4 us (level)
  no operation moved by 1% of the time
where the time goes in v8:
time: 31.4 us; the launch traced here: 31.2 us
  Pallas kernels  30.6 us (97%)
  local copies, waits for them, and re-layouts  0.61 us (2%)
    pallas_call x1, Pallas kernels, body(): pl.pallas_call(functools.partial(kernel, spaces, subs), out_shape=pltpu.V...  30.6 us

profile of v8, /device:TPU:1, one launch (start us, length us, event | category | flops | bytes accessed | tf_op | source)
XLA Modules:
  0.0 31.2 jit_solution(14678444958372668071)
XLA Ops:
  0.0 30.6 %shard_map.100 = f32[3,2,3,2,128]{4,3,2,1,0:T(2,128)S(1)} custom-call(f32[3,2,3,2,128]{4,3,2,1,0:T(2,128)} %bitcast.4, f32[2,3,2,128]{3,2,1,0:T(2,128)} %bitcast.5, s32[2,2,3]{2,1,0:T(2,128)} %count_hbm.1, bf16[512,128]{1,0:T(8,128)(2,1)} %constant.14.clone.place_hbm, bf16[256,1152]{1,0:T(8,128)(2,1)} %constant.15.clone.wide_hi_hbm, ...), custom_call_target="tpu_custom_call" | custom-call | tf_op jit(solution)/shard_map/pallas_call | solution.py:611
  30.6 0.6 %copy.12 = f32[3,2,2,3,128]{4,2,3,1,0:T(2,128)} copy(f32[3,2,2,3,128]{4,2,3,1,0:T(2,128)S(1)} %bitcast.3) | data formatting | bytes 36864
